TPU v7x, 32 devices: a whole 2x2x4 slice. The times are simulated.
32 devices in a mesh: lat: 4 (over x, core), lon: 8 (over z, y).
Axes of the slice: x: 2, y: 2, z: 4, core: 2. Of those that a mesh axis runs over, the one named last changes fastest.
Arguments:
- atmosphere_inputs: bfloat16 [9, 512, 1024], P(None, 'lat', 'lon'), may hold values from -6 to 6
- thermal_anomaly: float32 [64, 131072], P(None, ('lat', 'lon')), may hold values from -6 to 6
- mixing_rates: float32 [64, 131072], P(None, ('lat', 'lon')), may hold values from 0.1 to 10
- adjacency_table: int32 [6, 131072], P(None, ('lat', 'lon')), may hold values from 0 to 4351
- lateral_spread_factor: float32 [6, 131072], P(None, ('lat', 'lon')), may hold values from 0.02 to 0.15
- sent_vertices: int32 [256, 32], P(('lat', 'lon')), may hold values from 0 to 4095
- corner_parallel: int32 [4, 131072], P(None, ('lat', 'lon')), may hold values from 0 to 127, as said below
- corner_longitude: int32 [4, 131072], P(None, ('lat', 'lon')), may hold values from 0 to 1023, as said below
- corner_share: float32 [4, 131072], P(None, ('lat', 'lon')), as said below
- exchange_factor: float32 [9], replicated, may hold values from -3 to 3
- sensitivity_vector: float32 [64, 131072], P(None, ('lat', 'lon')), may hold values from -6 to 6
Outputs:
- updated_warmth: float32 [64, 131072], P(None, ('lat', 'lon'))
- temp_grad: float32 [64, 131072], P(None, ('lat', 'lon'))
- forcing_grad: float32 [9, 512, 1024], P(None, 'lat', 'lon')
Inputs may be any that keep to these rules, and one draw needn't show every extreme that they name: `adjacency_table`: entries below 4096 are the partition's own nodes; entry 4096 + c * 32 + h is the h-th halo node received from the c-th partition of its group. `sent_vertices`: row p * 8 + c lists local nodes of partition p sent to the c-th partition of its group. `corner_parallel`: the four stencil points of a node are rows r, r + 1, r, r + 1 of its latitude band. `corner_longitude`: the four stencil points of a node are columns c, c, c + 1, c + 1 taken modulo 1024; for a partition of lon index b all of them lie in the 256 columns from b * 128 - 128 / 2 on, taken modulo 1024, and both ends of that window are named by some node of every partition. `corner_share`: products (1 - u)(1 - v), u (1 - v), (1 - u) v, u v of the node's row fraction u and column fraction v.
All inputs are finite; a program needn't handle non-finite values.
Results may differ from a plain program's by a relative error of at most 0.00055.
Values may be sent and summed in bfloat16 or wider, within the bound.
A program may use at most 128 MiB of HBM per device.

v0:
```python
import jax
import jax.numpy as jnp
from jax import lax
from jax.sharding import PartitionSpec as P


def padded(cells, sides, width):
    for axis, dim in sides:
        count = lax.axis_size(axis)
        head = lax.slice_in_dim(cells, 0, width, axis=dim)
        tail = lax.slice_in_dim(cells, cells.shape[dim] - width, cells.shape[dim], axis=dim)
        cells = jnp.concatenate(
            [
                lax.ppermute(tail, axis, [(i, (i + 1) % count) for i in range(count)]),
                cells,
                lax.ppermute(head, axis, [((i + 1) % count, i) for i in range(count)]),
            ],
            axis=dim,
        )
    return cells


def column_solve(mixing_rates, source_vector):
    zero_row = jnp.zeros_like(mixing_rates[:1])
    prev_k = jnp.concatenate([zero_row, mixing_rates[:-1]], 0)
    above_k = jnp.concatenate([-mixing_rates[:-1], zero_row], 0)
    diagonal = 1.0 + prev_k + mixing_rates

    def sweep_down(carry, level_items):
        c_prev, d_prev = carry
        below_row, diag_row, above_row, rhs_row = level_items
        pivot = diag_row - below_row * c_prev
        c_next = above_row / pivot
        d_next = (rhs_row - below_row * d_prev) / pivot
        return ((c_next, d_next), (c_next, d_next))

    start = (jnp.zeros_like(mixing_rates[0]), jnp.zeros_like(mixing_rates[0]))
    _, (c_all, d_all) = lax.scan(sweep_down, start, (-prev_k, diagonal, above_k, source_vector))

    def sweep_up(x_next, level_items):
        c_row, d_row = level_items
        x_row = d_row - c_row * x_next
        return (x_row, x_row)

    _, solved = lax.scan(sweep_up, jnp.zeros_like(mixing_rates[0]), (c_all, d_all), reverse=True)
    return solved


def inner_portion(
    parallel_band,
    thermal_anomaly,
    extended_vertices,
    mixing_rates,
    adjacency_table,
    lateral_spread_factor,
    corner_position,
    corner_share,
    exchange_factor,
    sensitivity_vector,
):
    fields = parallel_band.shape[0]
    vertex_total = thermal_anomaly.shape[1]
    points = (
        jnp.take(parallel_band, corner_position.reshape(-1), axis=1)
        .astype(jnp.float32)
        .reshape(fields, 4, vertex_total)
    )
    driven_profile = jnp.sum(points * corner_share[None], 1)
    breeze_drive = jnp.sqrt(
        driven_profile[0] * driven_profile[0] + driven_profile[1] * driven_profile[1] + 1.0
    )
    boundary_transfer = jnp.sum(
        exchange_factor[:, None] * driven_profile, 0
    ) + 0.1 * breeze_drive * (driven_profile[2] - thermal_anomaly[0])
    gathered_entries = jnp.take(extended_vertices, adjacency_table, axis=1)
    source_vector = thermal_anomaly + jnp.sum(
        lateral_spread_factor[None] * (gathered_entries - thermal_anomaly[:, None, :]), 1
    )
    source_vector = source_vector.at[0].add(boundary_transfer)
    updated_warmth = column_solve(mixing_rates, source_vector)
    adjoint = column_solve(mixing_rates, sensitivity_vector)
    surface = adjoint[0]
    spread = lateral_spread_factor[None] * adjoint[:, None, :]
    ext_grad = jnp.zeros_like(extended_vertices).at[:, adjacency_table].add(spread)
    temp_grad = (
        adjoint * (1.0 - jnp.sum(lateral_spread_factor, 0))[None] + ext_grad[:, :vertex_total]
    )
    temp_grad = temp_grad.at[0].add(-0.1 * surface * breeze_drive)
    excess_quantity = 0.1 * (driven_profile[2] - thermal_anomaly[0]) / breeze_drive
    node_grad = surface[None] * exchange_factor[:, None]
    node_grad = node_grad.at[0].add(surface * excess_quantity * driven_profile[0])
    node_grad = node_grad.at[1].add(surface * excess_quantity * driven_profile[1])
    node_grad = node_grad.at[2].add(surface * 0.1 * breeze_drive)
    entries_list = (node_grad[:, None, :] * corner_share[None]).reshape(fields, 4 * vertex_total)
    return (updated_warmth, temp_grad, ext_grad[:, vertex_total:], entries_list)


def per_device(
    atmosphere_inputs,
    thermal_anomaly,
    mixing_rates,
    adjacency_table,
    lateral_spread_factor,
    sent_vertices,
    corner_parallel,
    corner_longitude,
    corner_share,
    exchange_factor,
    sensitivity_vector,
):
    layer_total = thermal_anomaly.shape[0]
    fields = atmosphere_inputs.shape[0]
    tile_rows = atmosphere_inputs.shape[1]
    tile_cols = atmosphere_inputs.shape[2]
    half_tile = tile_cols // 2
    columns = lax.axis_size("lon")
    halo_rows = sent_vertices.shape[1]
    band_width = tile_cols * columns
    window_width = 2 * tile_cols
    window_start = lax.axis_index("lon") * tile_cols - half_tile
    local_col = (corner_longitude - window_start) % band_width
    local_index = corner_parallel * window_width + local_col
    departing_border = jnp.take(thermal_anomaly, sent_vertices, axis=1)
    received_border = (
        lax.all_to_all(
            departing_border.astype(jnp.bfloat16), "lon", split_axis=1, concat_axis=1, tiled=True
        )
        .astype(departing_border.dtype)
        .reshape(layer_total, columns * halo_rows)
    )
    extended_vertices = jnp.concatenate([thermal_anomaly, received_border], 1)
    window = padded(atmosphere_inputs, (("lon", 2),), half_tile).reshape(
        fields, tile_rows * window_width
    )
    updated_warmth, owned_derivative, border_derivative, entries_list = inner_portion(
        window,
        thermal_anomaly,
        extended_vertices,
        mixing_rates,
        adjacency_table,
        lateral_spread_factor,
        local_index,
        corner_share,
        exchange_factor,
        sensitivity_vector,
    )
    back = lax.all_to_all(
        border_derivative.reshape(layer_total, columns, halo_rows).astype(jnp.bfloat16),
        "lon",
        split_axis=1,
        concat_axis=1,
        tiled=True,
    ).astype(jnp.float32)
    temp_grad = owned_derivative.at[:, sent_vertices].add(back)
    window_grad = (
        jnp.zeros((fields, tile_rows * window_width), jnp.float32)
        .at[:, local_index.reshape(-1)]
        .add(entries_list)
        .reshape(fields, tile_rows, window_width)
    )
    own_part = window_grad[:, :, half_tile : half_tile + tile_cols]
    widened = padded(window_grad, (("lon", 2),), half_tile)
    rims = jnp.concatenate([widened[:, :, :half_tile], widened[:, :, 5 * half_tile :]], 2)
    forcing_grad = own_part + rims
    return (updated_warmth, temp_grad, forcing_grad)


def solution(mesh):
    placed = (
        P(None, "lat", "lon"),
        P(None, ("lat", "lon")),
        P(None, ("lat", "lon")),
        P(None, ("lat", "lon")),
        P(None, ("lat", "lon")),
        P(("lat", "lon"), None),
        P(None, ("lat", "lon")),
        P(None, ("lat", "lon")),
        P(None, ("lat", "lon")),
        P(),
        P(None, ("lat", "lon")),
    )
    return jax.shard_map(
        per_device,
        mesh=mesh,
        in_specs=placed,
        out_specs=(P(None, ("lat", "lon")), P(None, ("lat", "lon")), P(None, "lat", "lon")),
        check_vma=False,
    )
```

profile of v0, /device:TPU:0, one launch (start us, length us, event | category | flops | bytes accessed | tf_op | source)
XLA Modules:
  0.0 982.5 jit_solution(18113749614061566199)
XLA Ops:
  0.7 2.1 fusion.23
  2.7 3.0 collective-permute-start
  5.7 3.0 collective-permute-start.1
  10.1 1.8 copy.73
  14.3 3.9 all-to-all-start
  19.8 1.6 pad_negate_fusion
  21.6 178.1 %while.75 = (s32[]{:T(128)}, f32[4096]{0:T(1024)S(1)}, f32[4096]{0:T(1024)S(1)}, f32[64,4096]{1,0:T(8,128)S(1)}, f32[64,4096]{1,0:T(8,128)S(1)}, /*index=5*/f32[...) while((s32[]{:T(128)}, f32[4096]{0:T(1024)S(1)}, ...), condition=%wide.region_8.9_spmd.clone, body=%wide.region_7.8_spmd.clone.sunk | while | flops 32771 | bytes 327815 | solution.py:38
  201.0 87.9 %while.76 = (s32[]{:T(128)}, f32[4096]{0:T(1024)S(1)}, f32[64,4096]{1,0:T(8,128)S(1)}, f32[64,4096]{1,0:T(8,128)}, f32[64,4096]{1,0:T(8,128)S(1)}, /*index=5*/s32[]{:T(128)}, s32[]{:T(128)}, s32[]{:T(128)}) while((s32[]{:T(128)}, f32[4096]{0:T(1024)S(1)}, f32[64,4096]{1,0:T(8,128)S(1)}, f32[64,4096]{1,0:T(8,128)}, ...), condition=%wide.region_10.11_spmd.clone, body=%wide.region_9.10_spmd.clone.sunk | while | flops 12292 | bytes 163955 | solution.py:45
  288.9 1.6 compare_and_fusion.1
  292.7 1.9 copy.81
  296.1 1.7 pad_maximum_fusion
  297.9 81.9 %gather_fusion.1 = f32[24576,64]{1,0:T(8,128)} fusion(f32[64,4352]{0,1:T(8,128)S(1)} %pad_maximum_fusion, s32[24576]{0:T(1024)S(1)} %broadcast_clamp_fusion), kind=kCustom, calls=%fused_computation.1 | custom fusion | bytes 12681216 | tf_op jit(solution)/shard_map/jit(_take)/gather | solution.py:75
  379.8 14.5 %broadcast_multiply_fusion = (f32[64,6,4096]{0,2,1:T(8,128)}, f32[64,4096]{0,1:T(8,128)}) fusion(f32[64,4096]{0,1:T(8,128)} %copy.81, f32[6,4096]{1,0:T(8,128)S(1)} %copy-done.8, f32[64,4096]{0,1:T(8,128)} %copy-done, f32[6,4096,64]{2,1,0:T(8,128)} %bitcast.103, pred[6,4096]{1,0:T(8,128)(4,1)} %compare_and_fusion), kind=kLoop, calls=%fused_computation.42 | loop fusion | flops 7602176 | bytes 15851520 | tf_op jit(solution)/shard_map/mul | solution.py:83
  394.3 131.4 %scatter_custom_fusion = f32[64,4352]{0,1:T(8,128)S(1)} fusion(s32[24576]{0:T(1024)} %copy-done.11, f32[24576,64]{1,0:T(8,128)} %bitcast.105, f32[]{:T(128)} %constant.295.clone.1), kind=kCustom, calls=%fused_computation.44 | custom fusion | flops 1572864 | bytes 1114624 | tf_op jit(solution)/shard_map/scatter-add | solution.py:84
  525.8 1.5 slice.162
  527.3 3.3 copy.90
  531.3 5.9 all-to-all-start.1
  537.2 2.3 multiply_add_fusion
  539.6 1.6 copy.75
  541.1 2.7 add.180
  544.1 1.5 pad_maximum_fusion.1
  545.6 6.2 copy.76
  551.7 59.9 %gather_fusion.2 = bf16[16384,9]{1,0:T(8,128)(2,1)} fusion(bf16[9,32768]{0,1:T(8,128)(2,1)} %bitcast.104, s32[16384]{0:T(1024)S(1)} %copy-done.15), kind=kCustom, calls=%fused_computation.2 | custom fusion | bytes 655360 | tf_op jit(solution)/shard_map/jit(_take)/gather | solution.py:64
  611.6 6.8 multiply_reduce_fusion
  618.5 1.3 copy.77
  619.8 1.8 broadcast_multiply_fusion.1
  621.6 1.2 slice_add_fusion.2
  622.8 1.6 scatter-add.50
  624.4 1.3 slice_add_fusion.1
  625.7 1.6 scatter-add.51
  627.3 1.0 slice_add_fusion
  628.3 1.6 scatter-add.52
  630.0 1.6 copy.84
  631.6 4.4 bitcast_multiply_fusion
  636.0 86.4 %scatter_custom_fusion.2 = f32[9,32768]{0,1:T(8,128)} fusion(s32[16384]{0:T(1024)} %bitcast.131, f32[9,16384]{0,1:T(8,128)} %bitcast_multiply_fusion, f32[]{:T(128)} %constant.295.clone.1), kind=kCustom, calls=%fused_computation.37 | custom fusion | flops 147456 | bytes 9568768 | tf_op jit(solution)/shard_map/scatter-add | solution.py:158
  722.4 8.4 fusion.21
  730.8 4.4 copy.92
  735.3 1.9 collective-permute-start.2
  737.2 4.5 copy.93
  741.7 2.8 collective-permute-start.3
  744.5 1.6 scatter-add.36
  746.2 182.1 %while.73 = (s32[]{:T(128)}, f32[4096]{0:T(1024)S(1)}, f32[4096]{0:T(1024)S(1)}, f32[64,4096]{1,0:T(8,128)S(1)}, f32[64,4096]{1,0:T(8,128)S(1)}, /*index=5*/f32[...) while((s32[]{:T(128)}, f32[4096]{0:T(1024)S(1)}, ...), condition=%wide.region_4.5_spmd.clone, body=%wide.region_3.4_spmd.clone.sunk | while | flops 32771 | bytes 327815 | solution.py:38
  747.2 1.0 constant_dynamic-slice_fusion.19
  750.1 1.0 constant_dynamic-slice_fusion.19
  752.9 1.0 constant_dynamic-slice_fusion.19
  755.8 1.0 constant_dynamic-slice_fusion.19
  764.3 1.0 constant_dynamic-slice_fusion.19
  767.2 1.0 constant_dynamic-slice_fusion.19
  770.0 1.0 constant_dynamic-slice_fusion.19
  772.9 1.0 constant_dynamic-slice_fusion.19
  781.4 1.0 constant_dynamic-slice_fusion.19
  784.2 1.0 constant_dynamic-slice_fusion.19
  787.1 1.0 constant_dynamic-slice_fusion.19
  789.9 1.0 constant_dynamic-slice_fusion.19
  798.5 1.0 constant_dynamic-slice_fusion.19
  801.3 1.0 constant_dynamic-slice_fusion.19
  804.2 1.0 constant_dynamic-slice_fusion.19
  928.4 30.4 %while.74 = (s32[]{:T(128)}, f32[4096]{0:T(1024)S(1)}, f32[64,4096]{1,0:T(8,128)S(1)}, f32[64,4096]{1,0:T(8,128)S(1)}, f32[64,4096]{1,0:T(8,128)S(1)}, /*index=5*/s32[]{:T(128)}, s32[]{:T(128)}, s32[]{:T(128)}) while((s32[]{:T(128)}, f32[4096]{0:T(1024)S(1)}, f32[64,4096]{1,0:T(8,128)S(1)}, f32[64,4096]{1,0:T(8,128)S(1)}, ...), condition=%wide.region_6.7_spmd.clone, body=%wide.region_5.6_spmd.clone.sunk | while | flops 12292 | bytes 163955 | solution.py:45
  959.8 7.8 slice.168
  967.6 7.4 copy.91
  976.1 2.7 scatter_fusion
  978.8 1.6 copy.88
  980.3 1.1 maximum_add_fusion
  981.5 1.1 copy.89
  (1101 shorter events, 465.6 us)
Async XLA Ops:
  0.6 17.6 %copy-start.9 = (s32[6,4096]{1,0:T(8,128)S(1)}, s32[6,4096]{1,0:T(8,128)}, u32[]{:S(2)}) copy-start(s32[6,4096]{1,0:T(8,128)} %param.32) | copy-start | bytes 294916
  0.6 19.0 %copy-start.3 = (f32[64,4096]{1,0:T(8,128)S(1)}, f32[64,4096]{1,0:T(8,128)}, u32[]{:S(2)}) copy-start(f32[64,4096]{1,0:T(8,128)} %param.31) | copy-start | bytes 3145732
  2.7 541.3 %collective-permute-start = (bf16[9,128,64]{2,1,0:T(8,128)(2,1)}, bf16[9,128,64]{2,1,0:T(8,128)(2,1)}, u32[]{:S(2)}, u32[]{:S(2)}) collective-permute-start(bf16[9,128,64]{2,1,0:T(8,128)(2,1)} %get-tuple-element.594), channel_id=1, source_target_pairs={{0,1},{1,2},{2,3},{3,4},{4,5},{5,6},{6,7},{7,0},{8,9},{9,10},{10,1... | collective-permute-start | bytes 442376 | tf_op jit(solution)/shard_map/ppermute | solution.py:14
  5.7 538.4 %collective-permute-start.1 = (bf16[9,128,64]{2,1,0:T(8,128)(2,1)}, bf16[9,128,64]{2,1,0:T(8,128)(2,1)}, u32[]{:S(2)}, u32[]{:S(2)}) collective-permute-start(bf16[9,128,64]{2,1,0:T(8,128)(2,1)} %get-tuple-element.595), channel_id=1, source_target_pairs={{1,0},{2,1},{3,2},{4,3},{5,4},{6,5},{7,6},{0,7},{9,8},{10,9},{11,1... | collective-permute-start | bytes 442376 | tf_op jit(solution)/shard_map/ppermute | solution.py:16
  11.9 9.5 copy-start
  12.0 0.7 copy-start.20
  14.3 280.9 %all-to-all-start = ((bf16[8,2,1024]{2,1,0:T(2,128)(2,1)}), bf16[8,2,1024]{2,1,0:T(2,128)(2,1)}, u32[]{:S(2)}, u32[]{:S(2)}) async-start(bf16[8,2,1024]{2,1,0:T(2,128)(2,1)} %reshape.272), calls=%async_computation | async-start | bytes 65536 | tf_op jit(solution)/shard_map/all_to_all | solution.py:125
  21.4 269.9 %copy-start.10 = (s32[6,4096]{1,0:T(8,128)S(1)}, s32[6,4096]{1,0:T(8,128)}, u32[]{:S(2)}) copy-start(s32[6,4096]{1,0:T(8,128)} %compare_select_fusion.1) | copy-start | bytes 294916
  21.4 270.0 %copy-start.8 = (f32[6,4096]{1,0:T(8,128)S(1)}, f32[6,4096]{1,0:T(8,128)}, u32[]{:S(2)}) copy-start(f32[6,4096]{1,0:T(8,128)} %param.33) | copy-start | bytes 294916
  199.7 1.0 copy-start.6
  199.7 1.3 copy-start.5
  200.7 93.9 %copy-start.12 = (f32[4,4096]{1,0:T(4,128)S(1)}, f32[4,4096]{1,0:T(4,128)}, u32[]{:S(2)}) copy-start(f32[4,4096]{1,0:T(4,128)} %param.37) | copy-start | bytes 196612
  290.6 5.4 copy-start.16
  291.4 4.7 copy-start.11
  525.8 11.4 %copy-start.17 = (f32[4096]{0:T(1024)S(1)}, f32[4096]{0:T(1024)}, u32[]{:S(2)}) copy-start(f32[4096]{0:T(1024)} %broadcast_subtract_fusion) | copy-start | bytes 49156
  527.3 12.3 %copy-start.1 = (f32[64,4096]{0,1:T(8,128)S(1)}, f32[64,4096]{0,1:T(8,128)}, u32[]{:S(2)}) copy-start(f32[64,4096]{0,1:T(8,128)} %get-tuple-element.599) | copy-start | bytes 3145732
  531.3 12.6 %all-to-all-start.1 = ((bf16[8,2,1024]{2,1,0:T(2,128)(2,1)}), bf16[8,2,1024]{2,1,0:T(2,128)(2,1)S(1)}, u32[]{:S(2)}, u32[]{:S(2)}) async-start(bf16[8,2,1024]{2,1,0:T(2,128)(2,1)} %reshape.274), calls=%async_computation.1 | async-start | bytes 65536 | tf_op jit(solution)/shard_map/all_to_all | solution.py:147
  545.5 6.2 copy-start.15
  551.7 59.9 %copy-start.13 = (f32[4,4096]{1,0:T(4,128)S(1)}, f32[4,4096]{1,0:T(4,128)}, u32[]{:S(2)}) copy-start(f32[4,4096]{1,0:T(4,128)} %param.37) | copy-start | bytes 196612
  551.7 59.9 %copy-start.18 = (pred[4,4096]{1,0:T(4,128)(4,1)S(1)}, pred[4,4096]{1,0:T(4,128)(4,1)}, u32[]{:S(2)}) copy-start(pred[4,4096]{1,0:T(4,128)(4,1)} %get-tuple-element.568) | copy-start | bytes 49156
  611.6 8.2 copy-start.19
  611.6 8.2 copy-start.22
  618.5 13.1 %copy-start.14 = (f32[1,32,4,128]{3,1,2,0:T(8,128)S(1)}, f32[1,32,4,128]{3,1,2,0:T(8,128)}, u32[]{:S(2)}) copy-start(f32[1,32,4,128]{3,1,2,0:T(8,128)} %copy.95) | copy-start | bytes 196612
  735.3 245.0 %collective-permute-start.2 = (f32[9,128,64]{1,2,0:T(8,128)}, f32[9,128,64]{1,2,0:T(8,128)}, u32[]{:S(2)}, u32[]{:S(2)}) collective-permute-start(f32[9,128,64]{1,2,0:T(8,128)} %copy.92), channel_id=1, source_target_pairs={{0,1},{1,2},{2,3},{3,4},{4,5},{5,6},{6,7},{7,0},{8,9},{9,10},{10,1... | collective-permute-start | bytes 884744 | tf_op jit(solution)/shard_map/ppermute | solution.py:14
  741.7 238.6 %collective-permute-start.3 = (f32[9,128,64]{1,2,0:T(8,128)}, f32[9,128,64]{1,2,0:T(8,128)}, u32[]{:S(2)}, u32[]{:S(2)}) collective-permute-start(f32[9,128,64]{1,2,0:T(8,128)} %copy.93), channel_id=1, source_target_pairs={{1,0},{2,1},{3,2},{4,3},{5,4},{6,5},{7,6},{0,7},{9,8},{10,9},{11,1... | collective-permute-start | bytes 884744 | tf_op jit(solution)/shard_map/ppermute | solution.py:16
  958.9 1.0 copy-start.7
  967.6 7.4 copy-start.2
  967.6 8.4 copy-start.21
  976.0 4.3 copy-start.4
where the time goes:
time: 990 us; the launch traced here: 983 us
  local copies, waits for them, and re-layouts  678 us (68%)
  other arithmetic  271 us (27%)
  starting transfers between devices  20.5 us (2%)
  loops' own time  11.4 us (1%)
    dynamic_slice x384, local copies, waits for them, and re-layouts, column_solve(): lax.scan(sweep_down, start, (-prev_k, diagonal, above_k, source_vector))  313 us
    dynamic_update_slice x384, local copies, waits for them, and re-layouts, column_solve(): lax.scan(sweep_down, start, (-prev_k, diagonal, above_k, source_vector))  151 us
    scatter-add x1, other arithmetic, inner_portion(): jnp.zeros_like(extended_vertices).at[:, adjacency_table].add(spread)  131 us
    scatter-add x1, other arithmetic, per_device(): window_grad = jnp.zeros((fields, tile_rows * window_width), jnp.float32)....  86.4 us
    gather x1, local copies, waits for them, and re-layouts, inner_portion(): gathered_entries = jnp.take(extended_vertices, adjacency_table, axis=1)  81.9 us
    gather x1, local copies, waits for them, and re-layouts, inner_portion(): jnp.take(parallel_band, corner_position.reshape(-1), axis=1)  59.9 us
    unnamed x59, local copies, waits for them, and re-layouts  30.2 us
  transfers between devices with their start and end apart: 6, of which 1 were waited for; matrix products, arithmetic and copies ran while one was open for 76% of the time, Pallas kernels for 0%

commit v1 on v0

v1 whole, which is shorter than its diff:
```python
import functools

import jax
import jax.numpy as jnp
from jax import lax
from jax.experimental import pallas as pl
from jax.experimental.pallas import tpu as pltpu
from jax.sharding import PartitionSpec as P

F32 = jnp.float32
BF16 = jnp.bfloat16
VMEM_BYTES = 56 * 1024 * 1024
LANES = 128
SLOT_ROWS = 256
NODE_TILE = 512


def whole(count):
    return [pl.BlockSpec(memory_space=pltpu.VMEM)] * count


def halves(value):
    high = lax.reduce_precision(value, 8, 7)
    return high.astype(BF16), (value - high).astype(BF16)


def adjoint_kernel(mix_ref, rhs_ref, x_ref, gain_ref, scale_ref, carry_ref):
    layers = mix_ref.shape[0]
    zero = jnp.zeros(mix_ref.shape[1:], F32)

    def down(level, state):
        mix_prev, gain_prev, d_prev = state
        mix = mix_ref[level]
        scale = 1.0 / (1.0 + mix + mix_prev * (1.0 - gain_prev))
        gain = mix * scale
        carry = mix_prev * scale
        d_next = rhs_ref[level] * scale + carry * d_prev
        gain_ref[level] = gain
        scale_ref[level] = scale
        carry_ref[level] = carry
        x_ref[level] = d_next
        return mix, gain, d_next

    lax.fori_loop(0, layers, down, (zero, zero, zero), unroll=4)

    def up(step, x_next):
        level = layers - 1 - step
        x_here = x_ref[level] + gain_ref[level] * x_next
        x_ref[level] = x_here
        return x_here

    lax.fori_loop(0, layers, up, zero, unroll=8)


def forward_kernel(rhs_ref, gain_ref, scale_ref, carry_ref, x_ref):
    layers = rhs_ref.shape[0]
    zero = jnp.zeros(rhs_ref.shape[1:], F32)

    def down(level, d_prev):
        d_next = rhs_ref[level] * scale_ref[level] + carry_ref[level] * d_prev
        x_ref[level] = d_next
        return d_next

    lax.fori_loop(0, layers, down, zero, unroll=8)

    def up(step, x_next):
        level = layers - 1 - step
        x_here = x_ref[level] + gain_ref[level] * x_next
        x_ref[level] = x_here
        return x_here

    lax.fori_loop(0, layers, up, zero, unroll=8)


def lateral_kernel(adj_ref, coef_ref, ext_ref, adjoint_ref, spread_ref, grad_ref, merged_ref):
    step = pl.program_id(0)
    slots, nodes = adj_ref.shape
    layers = grad_ref.shape[0]

    @pl.when(step == 0)
    def _():
        for k in range(slots):
            same = coef_ref[k : k + 1, :]
            for m in range(slots):
                if m != k:
                    equal = adj_ref[k : k + 1, :] == adj_ref[m : m + 1, :]
                    same = same + jnp.where(equal, coef_ref[m : m + 1, :], 0.0)
            merged_ref[k : k + 1, :] = same

    row = lax.broadcasted_iota(jnp.int32, (SLOT_ROWS, NODE_TILE), 0).astype(F32).astype(BF16)
    ext = ext_ref[...]
    total = jnp.zeros((2 * layers, SLOT_ROWS), F32)
    fine = jnp.zeros((layers, SLOT_ROWS), F32)
    for tile in range(nodes // NODE_TILE):
        cols = pl.ds(tile * NODE_TILE, NODE_TILE)
        local = (adj_ref[:, cols] - step * SLOT_ROWS).astype(F32).astype(BF16)
        share, rest = halves(merged_ref[:, cols])
        weights = jnp.zeros((SLOT_ROWS, NODE_TILE), BF16)
        small = jnp.zeros((SLOT_ROWS, NODE_TILE), BF16)
        for k in range(slots):
            here = row == local[k : k + 1, :]
            weights = jnp.where(here, share[k : k + 1, :], weights)
            small = jnp.where(here, rest[k : k + 1, :], small)
        part = jnp.dot(ext, weights, preferred_element_type=F32)
        part = part[:layers] + part[layers:]
        part += jnp.dot(ext[:layers], small, preferred_element_type=F32)

        @pl.when(step == 0)
        def _(part=part, cols=cols):
            spread_ref[:, cols] = part

        @pl.when(step > 0)
        def _(part=part, cols=cols):
            spread_ref[:, cols] += part

        contract = (((1,), (1,)), ((), ()))
        total += lax.dot_general(
            adjoint_ref[:, cols], weights, contract, preferred_element_type=F32
        )
        fine += lax.dot_general(
            adjoint_ref[:layers, cols], small, contract, preferred_element_type=F32
        )
    grad_ref[...] = total[:layers] + total[layers:] + fine


def forcing_kernel(
    start_ref,
    factor_ref,
    window_ref,
    row_ref,
    col_ref,
    share_ref,
    surface_ref,
    thermal_ref,
    flux_ref,
    corr_ref,
    grad_ref,
    *,
    band_width,
):
    fields, tile_rows, window_cols = grad_ref.shape
    tile = row_ref.shape[1]

    @pl.when(pl.program_id(0) == 0)
    def _():
        grad_ref[...] = jnp.zeros_like(grad_ref)

    share = share_ref[...]
    row_low = share[0:1] + share[2:3]
    row_high = share[1:2] + share[3:4]
    col_low = share[0:1] + share[1:2]
    col_high = share[2:3] + share[3:4]
    base_row = row_ref[0:1, :]
    base_col = col_ref[0:1, :] - start_ref[0]
    base_col = jnp.where(base_col < 0, base_col + band_width, base_col)
    base_col = jnp.where(base_col >= band_width, base_col - band_width, base_col)
    row_at = lax.broadcasted_iota(jnp.int32, (tile_rows, tile), 0)
    col_at = lax.broadcasted_iota(jnp.int32, (window_cols, tile), 0)
    rows = jnp.where(
        row_at == base_row, row_low, jnp.where(row_at == base_row + 1, row_high, 0.0)
    )
    cols = jnp.where(
        col_at == base_col, col_low, jnp.where(col_at == base_col + 1, col_high, 0.0)
    )
    cols_hi, cols_lo = halves(cols)
    forced = []
    for f in range(fields):
        field = window_ref[f]
        mixed = jnp.dot(field, cols_hi, preferred_element_type=F32)
        mixed = mixed + jnp.dot(field, cols_lo, preferred_element_type=F32)
        forced.append(jnp.sum(mixed * rows, axis=0, keepdims=True))
    wind = jnp.sqrt(forced[0] * forced[0] + forced[1] * forced[1] + 1.0)
    excess = forced[2] - thermal_ref[...]
    flux = 0.1 * wind * excess
    for f in range(fields):
        flux = flux + factor_ref[f] * forced[f]
    flux_ref[...] = flux
    surface = surface_ref[...]
    corr_ref[...] = -0.1 * surface * wind
    quotient = surface * (0.1 * excess / wind)
    contract = (((1,), (1,)), ((), ()))
    for f in range(fields):
        node_grad = surface * factor_ref[f]
        if f < 2:
            node_grad = node_grad + quotient * forced[f]
        if f == 2:
            node_grad = node_grad + 0.1 * surface * wind
        left_hi, left_lo = halves(node_grad * rows)
        dot = functools.partial(
            lax.dot_general, dimension_numbers=contract, preferred_element_type=F32
        )
        grad_ref[f] += dot(left_hi, cols_hi) + dot(left_lo, cols_hi) + dot(left_hi, cols_lo)


def cost(flops, moved):
    return pl.CostEstimate(flops=flops, bytes_accessed=moved, transcendentals=0)


def per_device(
    atmosphere_inputs,
    thermal_anomaly,
    mixing_rates,
    adjacency_table,
    lateral_spread_factor,
    sent_vertices,
    corner_parallel,
    corner_longitude,
    corner_share,
    exchange_factor,
    sensitivity_vector,
):
    layers, nodes = thermal_anomaly.shape
    fields, tile_rows, tile_cols = atmosphere_inputs.shape
    half = tile_cols // 2
    columns = lax.axis_size("lon")
    halo = columns * sent_vertices.shape[1]
    slots = adjacency_table.shape[0]
    band_width = tile_cols * columns
    window_cols = 2 * tile_cols
    extended = nodes + halo
    params = pltpu.CompilerParams(vmem_limit_bytes=VMEM_BYTES)
    upward = [(i, (i + 1) % columns) for i in range(columns)]
    downward = [((i + 1) % columns, i) for i in range(columns)]
    start = (lax.axis_index("lon") * tile_cols - half).astype(jnp.int32).reshape(1)

    from_left = lax.ppermute(atmosphere_inputs[:, :, tile_cols - half :], "lon", upward)
    from_right = lax.ppermute(atmosphere_inputs[:, :, :half], "lon", downward)

    node_at = lax.broadcasted_iota(jnp.int32, (halo, nodes), 1)
    chosen = (sent_vertices.reshape(halo, 1) == node_at).astype(BF16)
    departing = lax.dot_general(
        chosen,
        thermal_anomaly.astype(BF16),
        (((1,), (1,)), ((), ())),
        preferred_element_type=F32,
    ).astype(BF16)
    received = lax.all_to_all(
        departing.reshape(columns, halo // columns, layers),
        "lon",
        split_axis=0,
        concat_axis=0,
        tiled=True,
    ).reshape(halo, layers)

    dense = (layers, nodes // LANES, LANES)
    block = jax.ShapeDtypeStruct(dense, F32)
    adjoint3, gain, scale, carry = pl.pallas_call(
        adjoint_kernel,
        out_shape=(block,) * 4,
        in_specs=whole(2),
        out_specs=tuple(whole(4)),
        compiler_params=params,
        cost_estimate=cost(layers * nodes * 20, layers * nodes * 24),
        name="adjoint_solve",
    )(mixing_rates.reshape(dense), sensitivity_vector.reshape(dense))
    adjoint = adjoint3.reshape(layers, nodes)
    surface = adjoint3[0].reshape(1, nodes)

    window = jnp.concatenate([from_left, atmosphere_inputs, from_right], 2)
    line = pl.BlockSpec((1, NODE_TILE), lambda i: (0, i))
    four = pl.BlockSpec((4, NODE_TILE), lambda i: (0, i))
    flux, corr, window_grad = pl.pallas_call(
        functools.partial(forcing_kernel, band_width=band_width),
        grid=(nodes // NODE_TILE,),
        out_shape=(
            jax.ShapeDtypeStruct((1, nodes), F32),
            jax.ShapeDtypeStruct((1, nodes), F32),
            jax.ShapeDtypeStruct((fields, tile_rows, window_cols), F32),
        ),
        in_specs=[
            pl.BlockSpec(memory_space=pltpu.SMEM),
            pl.BlockSpec(memory_space=pltpu.SMEM),
            pl.BlockSpec((fields, tile_rows, window_cols), lambda i: (0, 0, 0)),
            four,
            four,
            four,
            line,
            line,
        ],
        out_specs=(
            line,
            line,
            pl.BlockSpec((fields, tile_rows, window_cols), lambda i: (0, 0, 0)),
        ),
        compiler_params=params,
        cost_estimate=cost(10 * fields * tile_rows * window_cols * nodes, 4000000),
        name="forcing",
    )(
        start,
        exchange_factor,
        window,
        corner_parallel,
        corner_longitude,
        corner_share,
        surface,
        thermal_anomaly[0:1],
    )
    rim_from_left = lax.ppermute(window_grad[:, :, window_cols - half :], "lon", upward)
    rim_from_right = lax.ppermute(window_grad[:, :, :half], "lon", downward)

    thermal_hi, thermal_lo = halves(thermal_anomaly)
    received = received.T
    ext = jnp.concatenate(
        [
            jnp.concatenate([thermal_hi, received], 1),
            jnp.concatenate([thermal_lo, jnp.zeros_like(received)], 1),
        ],
        0,
    )
    spread, grad = pl.pallas_call(
        lateral_kernel,
        grid=(extended // SLOT_ROWS,),
        out_shape=(
            jax.ShapeDtypeStruct((layers, nodes), F32),
            jax.ShapeDtypeStruct((layers, extended), F32),
        ),
        in_specs=[
            pl.BlockSpec((slots, nodes), lambda i: (0, 0)),
            pl.BlockSpec((slots, nodes), lambda i: (0, 0)),
            pl.BlockSpec((2 * layers, SLOT_ROWS), lambda i: (0, i)),
            pl.BlockSpec((2 * layers, nodes), lambda i: (0, 0)),
        ],
        out_specs=(
            pl.BlockSpec((layers, nodes), lambda i: (0, 0)),
            pl.BlockSpec((layers, SLOT_ROWS), lambda i: (0, i)),
        ),
        scratch_shapes=[pltpu.VMEM((slots, nodes), F32)],
        compiler_params=params,
        cost_estimate=cost(8 * layers * nodes * extended, 8000000),
        name="lateral",
    )(
        adjacency_table,
        lateral_spread_factor,
        ext,
        jnp.concatenate(halves(adjoint), 0),
    )
    halo_grad = grad[:, nodes:].astype(BF16).T
    back = lax.all_to_all(
        halo_grad.reshape(columns, halo // columns, layers),
        "lon",
        split_axis=0,
        concat_axis=0,
        tiled=True,
    ).reshape(halo, layers)

    keep = 1.0 - jnp.sum(lateral_spread_factor, 0, keepdims=True)
    top = lax.broadcasted_iota(jnp.int32, (layers, nodes), 0) == 0
    rhs = thermal_anomaly * keep + spread + jnp.where(top, flux, 0.0)
    updated = pl.pallas_call(
        forward_kernel,
        out_shape=block,
        in_specs=whole(4),
        out_specs=pl.BlockSpec(memory_space=pltpu.VMEM),
        compiler_params=params,
        cost_estimate=cost(layers * nodes * 6, layers * nodes * 20),
        name="forward_solve",
    )(rhs.reshape(dense), gain, scale, carry)
    updated_warmth = updated.reshape(layers, nodes)

    returned = lax.dot_general(
        back, chosen, (((0,), (0,)), ((), ())), preferred_element_type=F32
    )
    temp_grad = adjoint * keep + grad[:, :nodes] + jnp.where(top, corr, 0.0) + returned
    forcing_grad = window_grad[:, :, half : half + tile_cols] + jnp.concatenate(
        [rim_from_left, rim_from_right], 2
    )
    return (updated_warmth, temp_grad, forcing_grad)


def solution(mesh):
    nodes = P(None, ("lat", "lon"))
    placed = (
        P(None, "lat", "lon"),
        nodes,
        nodes,
        nodes,
        nodes,
        P(("lat", "lon"), None),
        nodes,
        nodes,
        nodes,
        P(),
        nodes,
    )
    return jax.shard_map(
        per_device,
        mesh=mesh,
        in_specs=placed,
        out_specs=(nodes, nodes, P(None, "lat", "lon")),
        check_vma=False,
    )
```

time: 990 us -> 177 us (0.18)
  local copies, waits for them, and re-layouts: 678 us -> 17.6 us
  other arithmetic: 271 us -> 9.41 us
  Pallas kernels: 0 us -> 109 us
  waiting for transfers between devices: 0.09 us -> 13.3 us
  loops' own time: 11.4 us -> 0 us
    dynamic_slice x384 -> x0, local copies, waits for them, and re-layouts: 313 us -> none  [column_solve(): lax.scan(sweep_down, start, (-prev_k, diagonal, above_k, source_vector))]
    scatter-add x3 -> x0, other arithmetic: 221 us -> none  [the longest x1 131 us: inner_portion(): jnp.zeros_like(extended_vertices).at[:, adjacency_table].add(spread)]
    dynamic_update_slice x384 -> x0, local copies, waits for them, and re-layouts: 151 us -> none  [column_solve(): lax.scan(sweep_down, start, (-prev_k, diagonal, above_k, source_vector))]
    gather x3 -> x0, local copies, waits for them, and re-layouts: 143 us -> none  [the longest x1 81.9 us: inner_portion(): gathered_entries = jnp.take(extended_vertices, adjacency_table, axis=1)]
    pallas_call x0 -> x4, Pallas kernels: none -> 109 us  [the longest x1 72.3 us: per_device(): pl.pallas_call(lateral_kernel, grid=(extended // SLOT_ROWS,), out_shape=(...]
    unnamed x59 -> x28, local copies, waits for them, and re-layouts: 30.2 us -> 8.9 us
    mul x3 -> x0, other arithmetic: 20.7 us -> none  [the longest x1 14.5 us: inner_portion(): spread = lateral_spread_factor[None] * adjoint[:, None, :]]
    slice x6, local copies, waits for them, and re-layouts: 20.4 us -> 5.34 us  [the longest x2 1.92 us: per_device(): window_grad[:, :, window_cols - half:]]
  transfers between devices with their start and end apart: 6 -> 6, of which waited for: 1 -> 2; matrix products, arithmetic and copies ran while one was open for 76% -> 10% of each run, Pallas kernels for 0% -> 44%
where the time goes in v1:
time: 177 us; the launch traced here: 176 us
  Pallas kernels  109 us (62%)
  starting transfers between devices  20.1 us (11%)
  local copies, waits for them, and re-layouts  17.6 us (10%)
  waiting for transfers between devices  13.3 us (8%)
  other arithmetic  9.41 us (5%)
  matrix products  5.83 us (3%)
    pallas_call x1, Pallas kernels, per_device(): pl.pallas_call(lateral_kernel, grid=(extended // SLOT_ROWS,), out_shape=(...  72.3 us
    pallas_call x1, Pallas kernels, per_device(): pl.pallas_call(functools.partial(forcing_kernel, band_width=band_width),...  28.8 us
    unnamed x28, local copies, waits for them, and re-layouts  8.9 us
    all_to_all x1, starting transfers between devices, per_device(): lax.all_to_all(departing.reshape(columns, halo // columns, layers), 'lon'...  7.28 us
    all_to_all x1, waiting for transfers between devices, per_device(): lax.all_to_all(halo_grad.reshape(columns, halo // columns, layers), 'lon'...  6.68 us
    ppermute x1, waiting for transfers between devices, per_device(): rim_from_right = lax.ppermute(window_grad[:, :, :half], 'lon', downward)  6.56 us
    all_to_all x1, starting transfers between devices, per_device(): lax.all_to_all(halo_grad.reshape(columns, halo // columns, layers), 'lon'...  6 us
    ppermute x1, starting transfers between devices, per_device(): from_right = lax.ppermute(atmosphere_inputs[:, :, :half], 'lon', downward)  4.72 us
  transfers between devices with their start and end apart: 6, of which 2 were waited for; matrix products, arithmetic and copies ran while one was open for 10% of the time, Pallas kernels for 44%

profile of v1, /device:TPU:0, one launch (start us, length us, event | category | flops | bytes accessed | tf_op | source)
XLA Modules:
  0.0 176.1 jit_solution(7229455084835287910)
XLA Ops:
  0.6 0.0 copy-start.3
  0.6 0.8 eq.19
  1.4 0.0 copy-start.8
  1.4 0.5 copy-done.8
  2.0 0.0 copy-start
  2.0 2.2 %fusion.4 = bf16[256,64]{0,1:T(8,128)(2,1)S(1)} fusion(s32[256]{0:T(256)S(1)} %eq.19, f32[64,4096]{1,0:T(8,128)} %param.12), kind=kOutput, calls=%fused_computation.11 | convolution fusion | flops 135544832 | bytes 1082368 | tf_op jit(solution)/shard_map/dot_general | solution.py:231
  4.2 0.1 copy.17
  4.3 0.7 reshape.52
  5.0 7.3 %all-to-all-start = ((bf16[8,2,1024]{2,1,0:T(2,128)(2,1)}), bf16[8,2,1024]{2,1,0:T(2,128)(2,1)S(1)}, u32[]{:S(2)}, u32[]{:S(2)}) async-start(bf16[8,2,1024]{2,1,0:T(2,128)(2,1)} %reshape.52), calls=%async_computation | async-start | bytes 65536 | tf_op jit(solution)/shard_map/all_to_all | solution.py:237
  12.3 0.0 copy-done.3
  12.3 0.9 fusion.13
  13.2 0.0 copy-start.4
  13.2 4.7 %collective-permute-start.1 = (bf16[9,128,64]{2,1,0:T(8,128)(2,1)}, bf16[9,128,64]{2,1,0:T(8,128)(2,1)}, u32[]{:S(2)}, u32[]{:S(2)}) collective-permute-start(bf16[9,128,64]{2,1,0:T(8,128)(2,1)} %get-tuple-element.28), channel_id=1, source_target_pairs={{1,0},{2,1},{3,2},{4,3},{5,4},{6,5},{7,6},{0,7},{9,8},{10,9},{11,1... | collective-permute-start | bytes 442376 | tf_op jit(solution)/shard_map/ppermute | solution.py:227
  18.0 0.0 collective-permute-start
  18.0 0.0 copy-done
  18.0 0.2 reduce-precision_convert_fusion.1
  18.1 0.0 copy-start.5
  18.1 0.0 copy-done.4
  18.2 1.2 copy.24
  19.3 0.3 copy-done.5
  19.6 1.2 copy.25
  20.8 4.5 %adjoint_solve.1 = (f32[64,32,128]{2,1,0:T(8,128)}, f32[64,32,128]{2,1,0:T(8,128)}, f32[64,32,128]{2,1,0:T(8,128)}, f32[64,32,128]{2,1,0:T(8,128)}) custom-call(f32[64,32,128]{2,1,0:T(8,128)} %bitcast.38, f32[64,32,128]{2,1,0:T(8,128)} %bitcast.39), custom_call_target="tpu_custom_call" | custom-call | flops 5242880 | bytes 6291456 | tf_op jit(solution)/shard_map/adjoint_solve/pallas_call | solution.py:247
  25.2 1.8 %reduce-precision_convert_fusion = (bf16[64,4096]{1,0:T(8,128)(2,1)S(1)}, bf16[64,4096]{1,0:T(8,128)(2,1)S(1)}) fusion(f32[8,8,32,128]{3,2,1,0:T(8,128)} %bitcast.34), kind=kLoop, calls=%fused_computation.8 | loop fusion | flops 1048576 | bytes 2097152 | tf_op jit(solution)/shard_map/convert_element_type | solution.py:24
  27.1 0.0 copy-start.1
  27.1 1.1 pad_maximum_fusion.adjoint_ref
  28.1 0.9 reduce_sum.9
  29.1 0.0 copy-done.1
  29.1 0.6 slice.30
  29.7 0.6 slice.31.thermal_ref
  30.3 0.0 all-to-all-done
  30.3 0.1 reshape.53
  30.4 0.1 copy.18
  30.5 1.1 fusion.5.ext_ref
  31.6 72.3 %lateral.1 = (f32[64,4096]{1,0:T(8,128)}, f32[64,4352]{1,0:T(8,128)}) custom-call(s32[6,4096]{1,0:T(8,128)} %adj_ref.1, f32[6,4096]{1,0:T(8,128)} %coef_ref.1, bf16[128,4352]{1,0:T(8,128)(2,1)} %fusion.5.ext_ref, bf16[128,4096]{1,0:T(8,128)(2,1)} %pad_maximum_fusion.adjoint_ref), custom_call_target="tpu_custom_call" | custom-call | flops 9126805504 | bytes 8000000 | tf_op jit(solution)/shard_map/lateral/pallas_call | solution.py:310
  103.9 0.8 fusion.11
  104.8 0.1 copy.19
  104.9 0.7 reshape.54
  105.6 6.0 %all-to-all-start.1 = ((bf16[8,2,1024]{2,1,0:T(2,128)(2,1)}), bf16[8,2,1024]{2,1,0:T(2,128)(2,1)S(1)}, u32[]{:S(2)}, u32[]{:S(2)}) async-start(bf16[8,2,1024]{2,1,0:T(2,128)(2,1)} %reshape.54), calls=%async_computation.1 | async-start | bytes 65536 | tf_op jit(solution)/shard_map/all_to_all | solution.py:338
  111.6 6.7 %all-to-all-done.1 = bf16[8,2,1024]{2,1,0:T(2,128)(2,1)S(1)} async-done(((bf16[8,2,1024]{2,1,0:T(2,128)(2,1)}), bf16[8,2,1024]{2,1,0:T(2,128)(2,1)S(1)}, u32[]{:S(2)}, u32[]{:S(2)}) %all-to-all-start.1) | async-done | bytes 32800 | tf_op jit(solution)/shard_map/all_to_all | solution.py:338
  118.3 0.1 reshape.55
  118.4 0.0 collective-permute-done.1
  118.4 0.0 collective-permute-done
  118.4 2.2 %pad_maximum_fusion.1.window_ref = bf16[9,128,256]{2,1,0:T(8,128)(2,1)} fusion(bf16[9,128,64]{2,1,0:T(8,128)(2,1)} %collective-permute-done.1, bf16[9,128,128]{2,1,0:T(8,128)(2,1)S(1)} %copy-done.3, bf16[9,128,64]{2,1,0:T(8,128)(2,1)} %collective-permute-done), kind=kLoop, calls=%fused_computation.21 | loop fusion | flops 1769472 | bytes 1179648 | tf_op jit(solution)/shard_map/concatenate | solution.py:259
  120.7 0.0 copy-start.6
  120.7 28.8 %forcing.1 = (f32[1,4096]{1,0:T(1,128)}, f32[1,4096]{1,0:T(1,128)}, f32[9,128,256]{2,1,0:T(8,128)}) custom-call(s32[1]{0:T(128)} %bitcast.3.start_ref, f32[9]{0:T(128)} %factor_ref.1, bf16[9,128,256]{2,1,0:T(8,128)(2,1)} %pad_maximum_fusion.1.window_ref, s32[4,4096]{1,0:T(4,128)} %row_ref.1, s32[4,4096]{1,0:T(4,128)} %col_ref.1, f32[4,4096]{1,0:T(4,128)} %share_ref.1, ...), custom_call_target="tpu_custom_call" | custom-call | flops 12079595520 | bytes 4000000 | tf_op jit(solution)/shard_map/forcing/pallas_call | solution.py:262
  149.5 0.0 copy-done.6
  149.5 0.9 add_bitcast_fusion
  150.4 1.2 copy.27
  151.5 3.6 %forward_solve.1 = f32[64,32,128]{2,1,0:T(8,128)} custom-call(f32[64,32,128]{2,1,0:T(8,128)} %bitcast.36, f32[64,32,128]{2,1,0:T(8,128)} %get-tuple-element.15.gain_ref, f32[64,32,128]{2,1,0:T(8,128)} %get-tuple-element.16.scale_ref, f32[64,32,128]{2,1,0:T(8,128)} %get-tuple-element.17.carry_ref), custom_call_target="tpu_custom_call" | custom-call | flops 1572864 | bytes 5242880 | tf_op jit(solution)/shard_map/forward_solve/pallas_call | solution.py:349
  155.1 2.9 %copy.33 = f32[8,8,32,128]{3,1,2,0:T(8,128)} copy(f32[8,8,32,128]{3,2,1,0:T(8,128)} %bitcast.37) | data formatting | bytes 2097152
  158.0 0.0 copy-done.2
  158.0 1.0 fusion.12
  159.0 1.3 copy.21
  160.3 0.7 collective-permute-start.3
  161.0 0.9 copy.20
  162.0 1.3 collective-permute-start.2
  163.3 0.0 copy-done.7
  163.3 0.0 copy-done.9
  163.3 3.6 %convolution_add_fusion = f32[64,4096]{1,0:T(8,128)} fusion(bf16[256,64]{1,0:T(8,128)(2,1)S(1)} %bitcast.43, s32[256]{0:T(256)S(1)} %copy-done.9, f32[64,4352]{1,0:T(8,128)} %get-tuple-element.18, f32[8,8,32,128]{3,2,1,0:T(8,128)S(1)} %bitcast.35, f32[4096]{0:T(1024)S(1)} %bitcast.48, f32[4096]{0:T(1024)S(1)} %broadcast_subtract_fusion, ...), kind=kOutput, calls=%fused_computation | convolution fusion | flops 136577024 | bytes 3212352 | tf_op jit(solution)/shard_map/dot_general | solution.py:360
  166.9 6.6 %collective-permute-done.3 = f32[9,128,64]{1,2,0:T(8,128)} collective-permute-done((f32[9,128,64]{1,2,0:T(8,128)S(1)}, f32[9,128,64]{1,2,0:T(8,128)}, u32[]{:S(2)}, u32[]{:S(2)}) %collective-permute-start.3) | collective-permute-done | bytes 294944 | tf_op jit(solution)/shard_map/ppermute | solution.py:299
  173.5 1.2 copy.23
  174.7 0.0 collective-permute-done.2
  174.7 0.2 copy.22
  174.9 1.2 maximum_add_fusion
  (5 shorter events, 0.0 us)
Async XLA Ops:
  0.6 11.7 %copy-start.3 = (bf16[9,128,128]{2,1,0:T(8,128)(2,1)S(1)}, bf16[9,128,128]{2,1,0:T(8,128)(2,1)}, u32[]{:S(2)}) copy-start(bf16[9,128,128]{2,1,0:T(8,128)(2,1)} %param.11) | copy-start | bytes 884740
  1.4 0.5 copy-start.8
  2.0 16.0 %copy-start = (f32[64,4096]{1,0:T(8,128)S(1)}, f32[64,4096]{1,0:T(8,128)}, u32[]{:S(2)}) copy-start(f32[64,4096]{1,0:T(8,128)} %param.12) | copy-start | bytes 3145732
  5.0 25.3 %all-to-all-start = ((bf16[8,2,1024]{2,1,0:T(2,128)(2,1)}), bf16[8,2,1024]{2,1,0:T(2,128)(2,1)S(1)}, u32[]{:S(2)}, u32[]{:S(2)}) async-start(bf16[8,2,1024]{2,1,0:T(2,128)(2,1)} %reshape.52), calls=%async_computation | async-start | bytes 65536 | tf_op jit(solution)/shard_map/all_to_all | solution.py:237
  13.2 4.9 %copy-start.4 = (f32[64,4096]{1,0:T(8,128)S(1)}, f32[64,4096]{1,0:T(8,128)}, u32[]{:S(2)}) copy-start(f32[64,4096]{1,0:T(8,128)} %param.13) | copy-start | bytes 3145732
  13.2 105.2 %collective-permute-start.1 = (bf16[9,128,64]{2,1,0:T(8,128)(2,1)}, bf16[9,128,64]{2,1,0:T(8,128)(2,1)}, u32[]{:S(2)}, u32[]{:S(2)}) collective-permute-start(bf16[9,128,64]{2,1,0:T(8,128)(2,1)} %get-tuple-element.28), channel_id=1, source_target_pairs={{1,0},{2,1},{3,2},{4,3},{5,4},{6,5},{7,6},{0,7},{9,8},{10,9},{11,1... | collective-permute-start | bytes 442376 | tf_op jit(solution)/shard_map/ppermute | solution.py:227
  18.0 100.5 %collective-permute-start = (bf16[9,128,64]{2,1,0:T(8,128)(2,1)}, bf16[9,128,64]{2,1,0:T(8,128)(2,1)}, u32[]{:S(2)}, u32[]{:S(2)}) collective-permute-start(bf16[9,128,64]{2,1,0:T(8,128)(2,1)} %get-tuple-element.27), channel_id=1, source_target_pairs={{0,1},{1,2},{2,3},{3,4},{4,5},{5,6},{6,7},{7,0},{8,9},{9,10},{10,1... | collective-permute-start | bytes 442376 | tf_op jit(solution)/shard_map/ppermute | solution.py:226
  18.1 1.5 copy-start.5
  27.1 2.0 %copy-start.1 = (f32[64,32,128]{2,1,0:T(8,128)S(1)}, f32[64,32,128]{2,1,0:T(8,128)}, u32[]{:S(2)}) copy-start(f32[64,32,128]{2,1,0:T(8,128)} %get-tuple-element.12) | copy-start | bytes 3145732
  105.6 12.7 %all-to-all-start.1 = ((bf16[8,2,1024]{2,1,0:T(2,128)(2,1)}), bf16[8,2,1024]{2,1,0:T(2,128)(2,1)S(1)}, u32[]{:S(2)}, u32[]{:S(2)}) async-start(bf16[8,2,1024]{2,1,0:T(2,128)(2,1)} %reshape.54), calls=%async_computation.1 | async-start | bytes 65536 | tf_op jit(solution)/shard_map/all_to_all | solution.py:338
  120.7 28.8 %copy-start.6 = (f32[64,4096]{1,0:T(8,128)S(1)}, f32[64,4096]{1,0:T(8,128)}, u32[]{:S(2)}) copy-start(f32[64,4096]{1,0:T(8,128)} %get-tuple-element.13) | copy-start | bytes 3145732
  155.1 2.9 %copy-start.2 = (f32[9,128,256]{2,1,0:T(8,128)S(1)}, f32[9,128,256]{2,1,0:T(8,128)}, u32[]{:S(2)}) copy-start(f32[9,128,256]{2,1,0:T(8,128)} %get-tuple-element.20) | copy-start | bytes 3538948
  159.0 4.3 %copy-start.7 = (f32[1,4096]{1,0:T(1,128)S(1)}, f32[1,4096]{1,0:T(1,128)}, u32[]{:S(2)}) copy-start(f32[1,4096]{1,0:T(1,128)} %get-tuple-element.19) | copy-start | bytes 49156
  159.0 4.3 %copy-start.9 = (s32[256]{0:T(256)S(1)}, s32[256]{0:T(256)}, u32[]{:S(2)}) copy-start(s32[256]{0:T(256)} %copy-done.8) | copy-start | bytes 3076
  160.3 13.2 %collective-permute-start.3 = (f32[9,128,64]{1,2,0:T(8,128)S(1)}, f32[9,128,64]{1,2,0:T(8,128)}, u32[]{:S(2)}, u32[]{:S(2)}) collective-permute-start(f32[9,128,64]{1,2,0:T(8,128)S(1)} %copy.21), channel_id=1, source_target_pairs={{1,0},{2,1},{3,2},{4,3},{5,4},{6,5},{7,6},{0,7},{9,8},{10,9},{11,1... | collective-permute-start | bytes 884744 | tf_op jit(solution)/shard_map/ppermute | solution.py:299
  162.0 12.7 %collective-permute-start.2 = (f32[9,128,64]{1,2,0:T(8,128)}, f32[9,128,64]{1,2,0:T(8,128)S(1)}, u32[]{:S(2)}, u32[]{:S(2)}) collective-permute-start(f32[9,128,64]{1,2,0:T(8,128)} %copy.20), channel_id=1, source_target_pairs={{0,1},{1,2},{2,3},{3,4},{4,5},{5,6},{6,7},{7,0},{8,9},{9,10},{10,1... | collective-permute-start | bytes 884744 | tf_op jit(solution)/shard_map/ppermute | solution.py:298

commit v2 on v1

v2 whole, which is shorter than its diff:
```python
import functools

import jax
import jax.numpy as jnp
from jax import lax
from jax.experimental import pallas as pl
from jax.experimental.pallas import tpu as pltpu
from jax.sharding import PartitionSpec as P

F32 = jnp.float32
BF16 = jnp.bfloat16
VMEM_BYTES = 56 * 1024 * 1024
LANES = 128
SLOT_ROWS = 256
NODE_TILE = 256
FORCE_TILE = 512


def whole(count):
    return [pl.BlockSpec(memory_space=pltpu.VMEM)] * count


def halves(value):
    high = value.astype(BF16)
    return high, (value - high.astype(F32)).astype(BF16)


def spread_levels(source_ref, dense_ref):
    layers = dense_ref.shape[0]
    for level in range(0, layers, 8):
        dense_ref[level : level + 8] = source_ref[level : level + 8, :].reshape(
            (8,) + dense_ref.shape[1:]
        )


def sweep_up(x_ref, gain_ref, zero):
    layers = x_ref.shape[0]

    def up(step, x_next):
        level = layers - 1 - step
        x_here = x_ref[level] + gain_ref[level] * x_next
        x_ref[level] = x_here
        return x_here

    lax.fori_loop(0, layers, up, zero, unroll=8)


def adjoint_kernel(
    mix_ref, rhs_ref, parts_ref, surface_ref, gain_ref, scale_ref, carry_ref, mix3_ref, x_ref
):
    layers, nodes = mix_ref.shape
    zero = jnp.zeros(x_ref.shape[1:], F32)
    spread_levels(mix_ref, mix3_ref)
    spread_levels(rhs_ref, x_ref)

    def down(level, state):
        mix_prev, gain_prev, d_prev = state
        mix = mix3_ref[level]
        scale = 1.0 / (1.0 + mix + mix_prev * (1.0 - gain_prev))
        gain = mix * scale
        carry = mix_prev * scale
        d_next = x_ref[level] * scale + carry * d_prev
        gain_ref[level] = gain
        scale_ref[level] = scale
        carry_ref[level] = carry
        x_ref[level] = d_next
        return mix, gain, d_next

    lax.fori_loop(0, layers, down, (zero, zero, zero), unroll=4)
    sweep_up(x_ref, gain_ref, zero)
    for level in range(0, layers, 16):
        flat = x_ref[level : level + 16].reshape(16, nodes)
        if level == 0:
            surface_ref[...] = flat[0:1]
        high, low = halves(flat)
        parts_ref[level : level + 16, :] = high
        parts_ref[layers + level : layers + level + 16, :] = low


def forward_kernel(rhs_ref, flux_ref, gain_ref, scale_ref, carry_ref, out_ref, x_ref):
    layers, nodes = rhs_ref.shape
    zero = jnp.zeros(x_ref.shape[1:], F32)
    spread_levels(rhs_ref, x_ref)
    x_ref[0] = x_ref[0] + flux_ref[...].reshape(x_ref.shape[1:])

    def down(level, d_prev):
        d_next = x_ref[level] * scale_ref[level] + carry_ref[level] * d_prev
        x_ref[level] = d_next
        return d_next

    lax.fori_loop(0, layers, down, zero, unroll=8)
    sweep_up(x_ref, gain_ref, zero)
    for level in range(0, layers, 8):
        out_ref[level : level + 8, :] = x_ref[level : level + 8].reshape(8, nodes)


def lateral_kernel(
    adj_ref, coef_ref, thermal_ref, received_ref, parts_ref, rhs_ref, own_ref, halo_ref, merged_ref
):
    step = pl.program_id(0)
    slots, nodes = adj_ref.shape
    layers = rhs_ref.shape[0]
    own_steps = nodes // SLOT_ROWS
    contract = (((1,), (1,)), ((), ()))

    @pl.when(step == 0)
    def _():
        for k in range(slots):
            same = coef_ref[k : k + 1, :]
            for m in range(slots):
                if m != k:
                    equal = adj_ref[k : k + 1, :] == adj_ref[m : m + 1, :]
                    same = same + jnp.where(equal, coef_ref[m : m + 1, :], 0.0)
            merged_ref[k : k + 1, :] = same
        keep = 1.0 - jnp.sum(coef_ref[...], axis=0, keepdims=True)
        rhs_ref[...] = thermal_ref[...] * keep

    here = pl.ds(pl.multiple_of(jnp.minimum(step, own_steps - 1) * SLOT_ROWS, SLOT_ROWS), SLOT_ROWS)
    high, low = halves(thermal_ref[:, here])
    is_own = step < own_steps
    high = jnp.where(is_own, high, received_ref[...])
    low = jnp.where(is_own, low, jnp.zeros_like(low))
    ext = jnp.concatenate([high, low], 0)
    row = lax.broadcasted_iota(jnp.int32, (SLOT_ROWS, NODE_TILE), 0).astype(F32).astype(BF16)
    total = jnp.zeros((2 * layers, SLOT_ROWS), F32)
    fine = jnp.zeros((layers, SLOT_ROWS), F32)
    for tile in range(nodes // NODE_TILE):
        cols = pl.ds(tile * NODE_TILE, NODE_TILE)
        local = (adj_ref[:, cols] - step * SLOT_ROWS).astype(F32).astype(BF16)
        share, rest = halves(merged_ref[:, cols])
        weights = jnp.zeros((SLOT_ROWS, NODE_TILE), BF16)
        small = jnp.zeros((SLOT_ROWS, NODE_TILE), BF16)
        for k in range(slots):
            match = row == local[k : k + 1, :]
            weights = jnp.where(match, share[k : k + 1, :], weights)
            small = jnp.where(match, rest[k : k + 1, :], small)
        part = jnp.dot(ext, weights, preferred_element_type=F32)
        part = part[:layers] + part[layers:]
        rhs_ref[:, cols] += part + jnp.dot(ext[:layers], small, preferred_element_type=F32)
        total += lax.dot_general(
            parts_ref[:, cols], weights, contract, preferred_element_type=F32
        )
        fine += lax.dot_general(
            parts_ref[:layers, cols], small, contract, preferred_element_type=F32
        )
    grad = total[:layers] + total[layers:] + fine

    @pl.when(is_own)
    def _():
        keep = 1.0 - jnp.sum(coef_ref[:, here], axis=0, keepdims=True)
        whole_x = parts_ref[:layers, here].astype(F32) + parts_ref[layers:, here].astype(F32)
        own_ref[...] = whole_x * keep + grad

    @pl.when(jnp.logical_not(is_own))
    def _():
        halo_ref[...] = grad.T.astype(BF16)


def forcing_kernel(
    start_ref,
    factor_ref,
    window_ref,
    row_ref,
    col_ref,
    share_ref,
    surface_ref,
    thermal_ref,
    flux_ref,
    corr_ref,
    own_ref,
    left_ref,
    right_ref,
    grad_ref,
    *,
    band_width,
):
    fields, tile_rows, window_cols = grad_ref.shape
    half = left_ref.shape[2]
    tile = row_ref.shape[1]

    @pl.when(pl.program_id(0) == 0)
    def _():
        grad_ref[...] = jnp.zeros_like(grad_ref)

    share = share_ref[...]
    row_low = share[0:1] + share[2:3]
    row_high = share[1:2] + share[3:4]
    col_low = share[0:1] + share[1:2]
    col_high = share[2:3] + share[3:4]
    base_row = row_ref[0:1, :]
    base_col = col_ref[0:1, :] - start_ref[0]
    base_col = jnp.where(base_col < 0, base_col + band_width, base_col)
    base_col = jnp.where(base_col >= band_width, base_col - band_width, base_col)
    row_at = lax.broadcasted_iota(jnp.int32, (tile_rows, tile), 0)
    col_at = lax.broadcasted_iota(jnp.int32, (window_cols, tile), 0)
    rows = jnp.where(
        row_at == base_row, row_low, jnp.where(row_at == base_row + 1, row_high, 0.0)
    )
    cols = jnp.where(
        col_at == base_col, col_low, jnp.where(col_at == base_col + 1, col_high, 0.0)
    )
    cols_hi, cols_lo = halves(cols)
    window = window_ref[...].reshape(fields * tile_rows, window_cols)
    mixed = jnp.dot(window, cols_hi, preferred_element_type=F32)
    mixed = mixed + jnp.dot(window, cols_lo, preferred_element_type=F32)
    forced = [
        jnp.sum(mixed[f * tile_rows : (f + 1) * tile_rows] * rows, axis=0, keepdims=True)
        for f in range(fields)
    ]
    wind = jnp.sqrt(forced[0] * forced[0] + forced[1] * forced[1] + 1.0)
    excess = forced[2] - thermal_ref[...]
    flux = 0.1 * wind * excess
    for f in range(fields):
        flux = flux + factor_ref[f] * forced[f]
    flux_ref[...] = flux
    surface = surface_ref[...]
    corr_ref[...] = -0.1 * surface * wind
    quotient = surface * (0.1 * excess / wind)
    dot = functools.partial(
        lax.dot_general,
        dimension_numbers=(((1,), (1,)), ((), ())),
        preferred_element_type=F32,
    )
    lefts = []
    for f in range(fields):
        node_grad = surface * factor_ref[f]
        if f < 2:
            node_grad = node_grad + quotient * forced[f]
        if f == 2:
            node_grad = node_grad + 0.1 * surface * wind
        lefts.append(halves(node_grad * rows))
    left_hi = jnp.concatenate([high for high, _ in lefts], 0)
    left_lo = jnp.concatenate([low for _, low in lefts], 0)
    grad = dot(left_hi, cols_hi) + dot(left_lo, cols_hi) + dot(left_hi, cols_lo)
    grad_ref[...] += grad.reshape(fields, tile_rows, window_cols)

    @pl.when(pl.program_id(0) == pl.num_programs(0) - 1)
    def _():
        for f in range(fields):
            grad = grad_ref[f]
            left_ref[f] = grad[:, :half]
            right_ref[f] = grad[:, window_cols - half :]
            own_ref[f] = grad[:, half : window_cols - half]


def cost(flops, moved):
    return pl.CostEstimate(flops=flops, bytes_accessed=moved, transcendentals=0)


def per_device(
    atmosphere_inputs,
    thermal_anomaly,
    mixing_rates,
    adjacency_table,
    lateral_spread_factor,
    sent_vertices,
    corner_parallel,
    corner_longitude,
    corner_share,
    exchange_factor,
    sensitivity_vector,
):
    layers, nodes = thermal_anomaly.shape
    fields, tile_rows, tile_cols = atmosphere_inputs.shape
    half = tile_cols // 2
    columns = lax.axis_size("lon")
    halo = columns * sent_vertices.shape[1]
    slots = adjacency_table.shape[0]
    band_width = tile_cols * columns
    window_cols = 2 * tile_cols
    extended = nodes + halo
    params = pltpu.CompilerParams(vmem_limit_bytes=VMEM_BYTES)
    upward = [(i, (i + 1) % columns) for i in range(columns)]
    downward = [((i + 1) % columns, i) for i in range(columns)]
    start = (lax.axis_index("lon") * tile_cols - half).astype(jnp.int32).reshape(1)

    from_left = lax.ppermute(atmosphere_inputs[:, :, tile_cols - half :], "lon", upward)
    from_right = lax.ppermute(atmosphere_inputs[:, :, :half], "lon", downward)

    node_at = lax.broadcasted_iota(jnp.int32, (halo, nodes), 1)
    chosen = (sent_vertices.reshape(halo, 1) == node_at).astype(BF16)
    departing = lax.dot_general(
        chosen,
        thermal_anomaly.astype(BF16),
        (((1,), (1,)), ((), ())),
        preferred_element_type=F32,
    ).astype(BF16)
    received = lax.all_to_all(
        departing.reshape(columns, halo // columns, layers),
        "lon",
        split_axis=0,
        concat_axis=0,
        tiled=True,
    ).reshape(halo, layers)

    dense = (layers, nodes // LANES, LANES)
    block = jax.ShapeDtypeStruct(dense, F32)
    parts, surface, gain, scale, carry = pl.pallas_call(
        adjoint_kernel,
        out_shape=(
            jax.ShapeDtypeStruct((2 * layers, nodes), BF16),
            jax.ShapeDtypeStruct((1, nodes), F32),
            block,
            block,
            block,
        ),
        in_specs=whole(2),
        out_specs=tuple(whole(5)),
        scratch_shapes=[pltpu.VMEM(dense, F32), pltpu.VMEM(dense, F32)],
        compiler_params=params,
        cost_estimate=cost(layers * nodes * 20, layers * nodes * 24),
        name="adjoint_solve",
    )(mixing_rates, sensitivity_vector)

    own_steps = nodes // SLOT_ROWS
    rhs, own_grad, halo_grad = pl.pallas_call(
        lateral_kernel,
        grid=(extended // SLOT_ROWS,),
        out_shape=(
            jax.ShapeDtypeStruct((layers, nodes), F32),
            jax.ShapeDtypeStruct((layers, nodes), F32),
            jax.ShapeDtypeStruct((halo, layers), BF16),
        ),
        in_specs=[
            pl.BlockSpec((slots, nodes), lambda i: (0, 0)),
            pl.BlockSpec((slots, nodes), lambda i: (0, 0)),
            pl.BlockSpec((layers, nodes), lambda i: (0, 0)),
            pl.BlockSpec((layers, SLOT_ROWS), lambda i: (0, jnp.maximum(i - own_steps, 0))),
            pl.BlockSpec((2 * layers, nodes), lambda i: (0, 0)),
        ],
        out_specs=(
            pl.BlockSpec((layers, nodes), lambda i: (0, 0)),
            pl.BlockSpec((layers, SLOT_ROWS), lambda i: (0, jnp.minimum(i, own_steps - 1))),
            pl.BlockSpec((SLOT_ROWS, layers), lambda i: (jnp.maximum(i - own_steps, 0), 0)),
        ),
        scratch_shapes=[pltpu.VMEM((slots, nodes), F32)],
        compiler_params=params,
        cost_estimate=cost(8 * layers * nodes * extended, 8000000),
        name="lateral",
    )(
        adjacency_table,
        lateral_spread_factor,
        thermal_anomaly,
        received.T,
        parts,
    )
    back = lax.all_to_all(
        halo_grad.reshape(columns, halo // columns, layers),
        "lon",
        split_axis=0,
        concat_axis=0,
        tiled=True,
    ).reshape(halo, layers)

    window = jnp.concatenate([from_left, atmosphere_inputs, from_right], 2)
    line = pl.BlockSpec((1, FORCE_TILE), lambda i: (0, i))
    four = pl.BlockSpec((4, FORCE_TILE), lambda i: (0, i))

    def all_of(width):
        return pl.BlockSpec((fields, tile_rows, width), lambda i: (0, 0, 0))

    def grid_shape(width):
        return jax.ShapeDtypeStruct((fields, tile_rows, width), F32)

    flux, corr, own_forcing, left_rim, right_rim = pl.pallas_call(
        functools.partial(forcing_kernel, band_width=band_width),
        grid=(nodes // FORCE_TILE,),
        out_shape=(
            jax.ShapeDtypeStruct((1, nodes), F32),
            jax.ShapeDtypeStruct((1, nodes), F32),
            grid_shape(tile_cols),
            grid_shape(half),
            grid_shape(half),
        ),
        in_specs=[
            pl.BlockSpec(memory_space=pltpu.SMEM),
            pl.BlockSpec(memory_space=pltpu.SMEM),
            all_of(window_cols),
            four,
            four,
            four,
            line,
            line,
        ],
        out_specs=(line, line, all_of(tile_cols), all_of(half), all_of(half)),
        scratch_shapes=[pltpu.VMEM((fields, tile_rows, window_cols), F32)],
        compiler_params=params,
        cost_estimate=cost(8 * fields * tile_rows * window_cols * nodes, 4000000),
        name="forcing",
    )(
        start,
        exchange_factor,
        window,
        corner_parallel,
        corner_longitude,
        corner_share,
        surface,
        thermal_anomaly[0:1],
    )
    rim_from_left = lax.ppermute(right_rim, "lon", upward)
    rim_from_right = lax.ppermute(left_rim, "lon", downward)

    updated_warmth = pl.pallas_call(
        forward_kernel,
        out_shape=jax.ShapeDtypeStruct((layers, nodes), F32),
        in_specs=whole(5),
        out_specs=pl.BlockSpec(memory_space=pltpu.VMEM),
        scratch_shapes=[pltpu.VMEM(dense, F32)],
        compiler_params=params,
        cost_estimate=cost(layers * nodes * 6, layers * nodes * 20),
        name="forward_solve",
    )(rhs, flux, gain, scale, carry)

    returned = lax.dot_general(
        back, chosen, (((0,), (0,)), ((), ())), preferred_element_type=F32
    )
    top = lax.broadcasted_iota(jnp.int32, (layers, nodes), 0) == 0
    temp_grad = own_grad + jnp.where(top, corr, 0.0) + returned
    forcing_grad = own_forcing + jnp.concatenate([rim_from_left, rim_from_right], 2)
    return (updated_warmth, temp_grad, forcing_grad)


def solution(mesh):
    nodes = P(None, ("lat", "lon"))
    placed = (
        P(None, "lat", "lon"),
        nodes,
        nodes,
        nodes,
        nodes,
        P(("lat", "lon"), None),
        nodes,
        nodes,
        nodes,
        P(),
        nodes,
    )
    return jax.shard_map(
        per_device,
        mesh=mesh,
        in_specs=placed,
        out_specs=(nodes, nodes, P(None, "lat", "lon")),
        check_vma=False,
    )
```

time: 177 us -> 115 us (0.65)
  Pallas kernels: 109 us -> 74.6 us
  local copies, waits for them, and re-layouts: 17.6 us -> 7.85 us
  waiting for transfers between devices: 13.3 us -> 4.45 us
  other arithmetic: 9.41 us -> 2.21 us
    pallas_call x1, Pallas kernels: 72.3 us -> 44 us  [per_device(): pl.pallas_call(lateral_kernel, grid=(extended // SLOT_ROWS,), out_shape=(...]
    pallas_call x1, Pallas kernels: 28.8 us -> 21.8 us  [per_device(): pl.pallas_call(functools.partial(forcing_kernel, band_width=band_width),...]
    all_to_all x1, waiting for transfers between devices: 6.68 us -> 0.01 us  [per_device(): lax.all_to_all(halo_grad.reshape(columns, halo // columns, layers), 'lon'...]
    unnamed x28 -> x14, local copies, waits for them, and re-layouts: 8.9 us -> 2.54 us
    slice x4 -> x0, local copies, waits for them, and re-layouts: 3.81 us -> none  [the longest x2 1.92 us: per_device(): window_grad[:, :, window_cols - half:]]
    ppermute x2, starting transfers between devices: 2.07 us -> 4.81 us  [the longest x1 2.85 us: per_device(): rim_from_right = lax.ppermute(left_rim, 'lon', downward)]
    all_to_all x1, starting transfers between devices: 6 us -> 3.33 us  [per_device(): lax.all_to_all(halo_grad.reshape(columns, halo // columns, layers), 'lon'...]
    concatenate x2 -> x0, other arithmetic: 2.18 us -> none  [the longest x1 1.11 us: per_device(): jnp.concatenate([jnp.concatenate([thermal_hi, received], 1), jnp.concaten...]
  transfers between devices with their start and end apart: 6 -> 6, of which waited for: 2 -> 2; matrix products, arithmetic and copies ran while one was open for 10% -> 8% of each run, Pallas kernels for 44% -> 65%
where the time goes in v2:
time: 115 us; the launch traced here: 114 us
  Pallas kernels  74.6 us (65%)
  starting transfers between devices  20.3 us (18%)
  local copies, waits for them, and re-layouts  7.85 us (7%)
  waiting for transfers between devices  4.45 us (4%)
  matrix products  4.12 us (4%)
  other arithmetic  2.21 us (2%)
    pallas_call x1, Pallas kernels, per_device(): pl.pallas_call(lateral_kernel, grid=(extended // SLOT_ROWS,), out_shape=(...  44 us
    pallas_call x1, Pallas kernels, per_device(): pl.pallas_call(functools.partial(forcing_kernel, band_width=band_width),...  21.8 us
    all_to_all x1, starting transfers between devices, per_device(): lax.all_to_all(departing.reshape(columns, halo // columns, layers), 'lon'...  7.28 us
    pallas_call x1, Pallas kernels, per_device(): pl.pallas_call(adjoint_kernel, out_shape=(jax.ShapeDtypeStruct((2 * layer...  4.86 us
    pallas_call x1, Pallas kernels, per_device(): pl.pallas_call(forward_kernel, out_shape=jax.ShapeDtypeStruct((layers, no...  4.02 us
    all_to_all x1, starting transfers between devices, per_device(): lax.all_to_all(halo_grad.reshape(columns, halo // columns, layers), 'lon'...  3.33 us
    ppermute x1, starting transfers between devices, per_device(): rim_from_right = lax.ppermute(left_rim, 'lon', downward)  2.85 us
    ppermute x1, starting transfers between devices, per_device(): from_right = lax.ppermute(atmosphere_inputs[:, :, :half], 'lon', downward)  2.77 us
  transfers between devices with their start and end apart: 6, of which 2 were waited for; matrix products, arithmetic and copies ran while one was open for 8% of the time, Pallas kernels for 65%

profile of v2, /device:TPU:0, one launch (start us, length us, event | category | flops | bytes accessed | tf_op | source)
XLA Modules:
  0.0 114.3 jit_solution(12965336156014704536)
XLA Ops:
  0.6 0.0 copy-start
  0.6 0.8 eq.17
  1.4 2.1 %fusion.3 = bf16[256,64]{0,1:T(8,128)(2,1)S(1)} fusion(s32[256]{0:T(256)S(1)} %eq.17, f32[64,4096]{1,0:T(8,128)} %thermal_ref.1), kind=kOutput, calls=%fused_computation.5 | convolution fusion | flops 135544832 | bytes 1082368 | tf_op jit(solution)/shard_map/dot_general | solution.py:282
  3.6 0.1 copy.16
  3.7 0.7 reshape.28
  4.4 7.3 %all-to-all-start = ((bf16[8,2,1024]{2,1,0:T(2,128)(2,1)}), bf16[8,2,1024]{2,1,0:T(2,128)(2,1)S(1)}, u32[]{:S(2)}, u32[]{:S(2)}) async-start(bf16[8,2,1024]{2,1,0:T(2,128)(2,1)} %reshape.28), calls=%async_computation | async-start | bytes 65536 | tf_op jit(solution)/shard_map/all_to_all | solution.py:288
  11.7 0.0 copy-done
  11.7 0.2 fusion.5
  11.9 2.1 %collective-permute-start = (bf16[9,128,64]{2,1,0:T(8,128)(2,1)S(1)}, bf16[9,128,64]{2,1,0:T(8,128)(2,1)S(1)}, u32[]{:S(2)}, u32[]{:S(2)}) collective-permute-start(bf16[9,128,64]{2,1,0:T(8,128)(2,1)S(1)} %get-tuple-element.29), channel_id=1, source_target_pairs={{0,1},{1,2},{2,3},{3,4},{4,5},{5,6},{6,7},{7,0},{8,9},{9,10},{10,1... | collective-permute-start | bytes 442376 | tf_op jit(solution)/shard_map/ppermute | solution.py:277
  13.9 2.8 %collective-permute-start.1 = (bf16[9,128,64]{2,1,0:T(8,128)(2,1)S(1)}, bf16[9,128,64]{2,1,0:T(8,128)(2,1)S(1)}, u32[]{:S(2)}, u32[]{:S(2)}) collective-permute-start(bf16[9,128,64]{2,1,0:T(8,128)(2,1)S(1)} %get-tuple-element.30), channel_id=1, source_target_pairs={{1,0},{2,1},{3,2},{4,3},{5,4},{6,5},{7,6},{0,7},{9,8},{10,9},{11,1... | collective-permute-start | bytes 442376 | tf_op jit(solution)/shard_map/ppermute | solution.py:278
  16.7 1.5 %slice.11.thermal_ref = f32[1,4096]{1,0:T(1,128)} slice(f32[64,4096]{1,0:T(8,128)} %thermal_ref.1), slice={[0:1], [0:4096]} | slice | bytes 32768 | tf_op jit(solution)/shard_map/slice | solution.py:398
  18.2 4.9 %adjoint_solve.1 = (bf16[128,4096]{1,0:T(8,128)(2,1)}, f32[1,4096]{1,0:T(1,128)}, f32[64,32,128]{2,1,0:T(8,128)}, f32[64,32,128]{2,1,0:T(8,128)}, f32[64,32,128]{2,1,0:T(8,128)}) custom-call(f32[64,4096]{1,0:T(8,128)} %mix_ref.1, f32[64,4096]{1,0:T(8,128)} %rhs_ref.1), custom_call_target="tpu_custom_call" | custom-call | flops 5242880 | bytes 6291456 | tf_op jit(solution)/shard_map/adjoint_solve/pallas_call | solution.py:298
  23.1 0.0 all-to-all-done
  23.1 0.1 reshape.29
  23.2 0.7 copy.17
  23.9 44.0 %lateral.1 = (f32[64,4096]{1,0:T(8,128)}, f32[64,4096]{1,0:T(8,128)}, bf16[256,64]{1,0:T(8,128)(2,1)}) custom-call(s32[6,4096]{1,0:T(8,128)} %adj_ref.1, f32[6,4096]{1,0:T(8,128)} %coef_ref.1, f32[64,4096]{1,0:T(8,128)} %thermal_ref.1, bf16[64,256]{1,0:T(8,128)(2,1)} %bitcast.12, bf16[128,4096]{1,0:T(8,128)(2,1)} %get-tuple-element.16.parts_ref), custom_call_target="tpu_custom_call" | custom-call | flops 9126805504 | bytes 8000000 | tf_op jit(solution)/shard_map/lateral/pallas_call | solution.py:316
  67.9 1.6 %reshape.30 = bf16[8,2,1024]{2,1,0:T(2,128)(2,1)} reshape(bf16[8,32,64]{2,1,0:T(8,128)(2,1)} %bitcast.11) | data formatting | bytes 65536
  69.5 3.3 %all-to-all-start.1 = ((bf16[8,2,1024]{2,1,0:T(2,128)(2,1)}), bf16[8,2,1024]{2,1,0:T(2,128)(2,1)S(1)}, u32[]{:S(2)}, u32[]{:S(2)}) async-start(bf16[8,2,1024]{2,1,0:T(2,128)(2,1)} %reshape.30), calls=%async_computation.1 | async-start | bytes 65536 | tf_op jit(solution)/shard_map/all_to_all | solution.py:347
  72.8 0.0 collective-permute-done
  72.8 0.0 collective-permute-done.1
  72.8 1.2 %pad_maximum_fusion.window_ref = bf16[9,128,256]{2,1,0:T(8,128)(2,1)} fusion(bf16[9,128,64]{2,1,0:T(8,128)(2,1)S(1)} %collective-permute-done.1, bf16[9,128,128]{2,1,0:T(8,128)(2,1)S(1)} %copy-done, bf16[9,128,64]{2,1,0:T(8,128)(2,1)S(1)} %collective-permute-done), kind=kLoop, calls=%fused_computation.6 | loop fusion | flops 1769472 | bytes 1179648 | tf_op jit(solution)/shard_map/concatenate | solution.py:355
  74.0 21.8 %forcing.1 = (f32[1,4096]{1,0:T(1,128)}, f32[1,4096]{1,0:T(1,128)}, f32[9,128,128]{2,1,0:T(8,128)}, f32[9,128,64]{2,1,0:T(8,128)}, f32[9,128,64]{2,1,0:T(8,128)}) custom-call(s32[1]{0:T(128)} %bitcast.3.start_ref, f32[9]{0:T(128)} %factor_ref.1, bf16[9,128,256]{2,1,0:T(8,128)(2,1)} %pad_maximum_fusion.window_ref, s32[4,4096]{1,0:T(4,128)} %row_ref.1, ...), custom_call_target="tpu_custom_call" | custom-call | flops 9663676416 | bytes 4000000 | tf_op jit(solution)/shard_map/forcing/pallas_call | solution.py:365
  95.8 0.0 copy-start.2
  95.8 1.3 %copy.18 = f32[9,128,64]{1,2,0:T(8,128)S(1)} copy(f32[9,128,64]{2,1,0:T(8,128)} %get-tuple-element.27) | data formatting | bytes 589824 | tf_op jit(solution)/shard_map/forcing/pallas_call | solution.py:365
  97.1 2.0 %collective-permute-start.2 = (f32[9,128,64]{1,2,0:T(8,128)S(1)}, f32[9,128,64]{1,2,0:T(8,128)S(1)}, u32[]{:S(2)}, u32[]{:S(2)}) collective-permute-start(f32[9,128,64]{1,2,0:T(8,128)S(1)} %copy.18), channel_id=1, source_target_pairs={{0,1},{1,2},{2,3},{3,4},{4,5},{5,6},{6,7},{7,0},{8,9},{9,10},{10,1... | collective-permute-start | bytes 884744 | tf_op jit(solution)/shard_map/ppermute | solution.py:400
  99.1 0.0 copy-done.2
  99.1 0.2 copy.19
  99.3 2.9 %collective-permute-start.3 = (f32[9,128,64]{1,2,0:T(8,128)S(1)}, f32[9,128,64]{1,2,0:T(8,128)S(1)}, u32[]{:S(2)}, u32[]{:S(2)}) collective-permute-start(f32[9,128,64]{1,2,0:T(8,128)S(1)} %copy.19), channel_id=1, source_target_pairs={{1,0},{2,1},{3,2},{4,3},{5,4},{6,5},{7,6},{0,7},{9,8},{10,9},{11,1... | collective-permute-start | bytes 884744 | tf_op jit(solution)/shard_map/ppermute | solution.py:401
  102.1 0.0 all-to-all-done.1
  102.2 0.1 reshape.31
  102.3 0.0 copy-start.1
  102.3 0.0 copy-start.4
  102.3 4.0 %forward_solve.1 = f32[64,4096]{1,0:T(8,128)} custom-call(f32[64,4096]{1,0:T(8,128)} %get-tuple-element.17.rhs_ref, f32[1,4096]{1,0:T(1,128)} %get-tuple-element.19.flux_ref, f32[64,32,128]{2,1,0:T(8,128)} %get-tuple-element.20.gain_ref, f32[64,32,128]{2,1,0:T(8,128)} %get-tuple-element.21.scale_ref, f32[64,32,128]{2,1,0:T(8,128)} %get-tuple-element.22.carry_ref), custom_call_target="tpu_custom_call" | custom-call | flops 1572864 | bytes 5242880 | tf_op jit(solution)/shard_map/forward_solve/pallas_call | solution.py:403
  106.3 0.0 copy-done.1
  106.3 0.0 copy-done.4
  106.3 2.0 %convolution_add_fusion = f32[64,4096]{1,0:T(8,128)} fusion(bf16[256,64]{1,0:T(8,128)(2,1)S(1)} %bitcast.8, s32[256]{0:T(256)S(1)} %eq.17, f32[64,4096]{1,0:T(8,128)S(1)} %copy-done.1, f32[4096]{0:T(1024)S(1)} %bitcast.13, pred[64]{0:T(512)(128)(4,1)S(1)} %iota_compare_fusion.5), kind=kOutput, calls=%fused_computation | convolution fusion | flops 136052736 | bytes 2147392 | tf_op jit(solution)/shard_map/dot_general | solution.py:414
  108.3 0.0 copy-start.3
  108.3 2.2 %collective-permute-done.2 = f32[9,128,64]{1,2,0:T(8,128)S(1)} collective-permute-done((f32[9,128,64]{1,2,0:T(8,128)S(1)}, f32[9,128,64]{1,2,0:T(8,128)S(1)}, u32[]{:S(2)}, u32[]{:S(2)}) %collective-permute-start.2) | collective-permute-done | bytes 294944 | tf_op jit(solution)/shard_map/ppermute | solution.py:400
  110.5 0.2 copy.20
  110.8 2.2 %collective-permute-done.3 = f32[9,128,64]{1,2,0:T(8,128)S(1)} collective-permute-done((f32[9,128,64]{1,2,0:T(8,128)S(1)}, f32[9,128,64]{1,2,0:T(8,128)S(1)}, u32[]{:S(2)}, u32[]{:S(2)}) %collective-permute-start.3) | collective-permute-done | bytes 294944 | tf_op jit(solution)/shard_map/ppermute | solution.py:401
  113.0 0.2 copy.21
  113.2 0.0 copy-done.3
  113.2 1.0 maximum_add_fusion
  (1 shorter events, 0.0 us)
Async XLA Ops:
  0.6 11.1 %copy-start = (bf16[9,128,128]{2,1,0:T(8,128)(2,1)S(1)}, bf16[9,128,128]{2,1,0:T(8,128)(2,1)}, u32[]{:S(2)}) copy-start(bf16[9,128,128]{2,1,0:T(8,128)(2,1)} %param.11) | copy-start | bytes 884740
  4.4 18.7 %all-to-all-start = ((bf16[8,2,1024]{2,1,0:T(2,128)(2,1)}), bf16[8,2,1024]{2,1,0:T(2,128)(2,1)S(1)}, u32[]{:S(2)}, u32[]{:S(2)}) async-start(bf16[8,2,1024]{2,1,0:T(2,128)(2,1)} %reshape.28), calls=%async_computation | async-start | bytes 65536 | tf_op jit(solution)/shard_map/all_to_all | solution.py:288
  11.9 61.0 %collective-permute-start = (bf16[9,128,64]{2,1,0:T(8,128)(2,1)S(1)}, bf16[9,128,64]{2,1,0:T(8,128)(2,1)S(1)}, u32[]{:S(2)}, u32[]{:S(2)}) collective-permute-start(bf16[9,128,64]{2,1,0:T(8,128)(2,1)S(1)} %get-tuple-element.29), channel_id=1, source_target_pairs={{0,1},{1,2},{2,3},{3,4},{4,5},{5,6},{6,7},{7,0},{8,9},{9,10},{10,1... | collective-permute-start | bytes 442376 | tf_op jit(solution)/shard_map/ppermute | solution.py:277
  13.9 58.9 %collective-permute-start.1 = (bf16[9,128,64]{2,1,0:T(8,128)(2,1)S(1)}, bf16[9,128,64]{2,1,0:T(8,128)(2,1)S(1)}, u32[]{:S(2)}, u32[]{:S(2)}) collective-permute-start(bf16[9,128,64]{2,1,0:T(8,128)(2,1)S(1)} %get-tuple-element.30), channel_id=1, source_target_pairs={{1,0},{2,1},{3,2},{4,3},{5,4},{6,5},{7,6},{0,7},{9,8},{10,9},{11,1... | collective-permute-start | bytes 442376 | tf_op jit(solution)/shard_map/ppermute | solution.py:278
  69.5 32.7 %all-to-all-start.1 = ((bf16[8,2,1024]{2,1,0:T(2,128)(2,1)}), bf16[8,2,1024]{2,1,0:T(2,128)(2,1)S(1)}, u32[]{:S(2)}, u32[]{:S(2)}) async-start(bf16[8,2,1024]{2,1,0:T(2,128)(2,1)} %reshape.30), calls=%async_computation.1 | async-start | bytes 65536 | tf_op jit(solution)/shard_map/all_to_all | solution.py:347
  95.8 3.3 %copy-start.2 = (f32[9,128,64]{2,1,0:T(8,128)S(1)}, f32[9,128,64]{2,1,0:T(8,128)}, u32[]{:S(2)}) copy-start(f32[9,128,64]{2,1,0:T(8,128)} %get-tuple-element.28) | copy-start | bytes 884740
  97.1 13.4 %collective-permute-start.2 = (f32[9,128,64]{1,2,0:T(8,128)S(1)}, f32[9,128,64]{1,2,0:T(8,128)S(1)}, u32[]{:S(2)}, u32[]{:S(2)}) collective-permute-start(f32[9,128,64]{1,2,0:T(8,128)S(1)} %copy.18), channel_id=1, source_target_pairs={{0,1},{1,2},{2,3},{3,4},{4,5},{5,6},{6,7},{7,0},{8,9},{9,10},{10,1... | collective-permute-start | bytes 884744 | tf_op jit(solution)/shard_map/ppermute | solution.py:400
  99.3 13.7 %collective-permute-start.3 = (f32[9,128,64]{1,2,0:T(8,128)S(1)}, f32[9,128,64]{1,2,0:T(8,128)S(1)}, u32[]{:S(2)}, u32[]{:S(2)}) collective-permute-start(f32[9,128,64]{1,2,0:T(8,128)S(1)} %copy.19), channel_id=1, source_target_pairs={{1,0},{2,1},{3,2},{4,3},{5,4},{6,5},{7,6},{0,7},{9,8},{10,9},{11,1... | collective-permute-start | bytes 884744 | tf_op jit(solution)/shard_map/ppermute | solution.py:401
  102.3 4.0 %copy-start.1 = (f32[64,4096]{1,0:T(8,128)S(1)}, f32[64,4096]{1,0:T(8,128)}, u32[]{:S(2)}) copy-start(f32[64,4096]{1,0:T(8,128)} %get-tuple-element.23) | copy-start | bytes 3145732
  102.3 4.0 %copy-start.4 = (f32[1,4096]{1,0:T(1,128)S(1)}, f32[1,4096]{1,0:T(1,128)}, u32[]{:S(2)}) copy-start(f32[1,4096]{1,0:T(1,128)} %get-tuple-element.24) | copy-start | bytes 49156
  108.3 4.9 %copy-start.3 = (f32[9,128,128]{2,1,0:T(8,128)S(1)}, f32[9,128,128]{2,1,0:T(8,128)}, u32[]{:S(2)}) copy-start(f32[9,128,128]{2,1,0:T(8,128)} %get-tuple-element.26) | copy-start | bytes 1769476

commit v3 on v2

--- a/solution.py
+++ b/solution.py
@@ -43,6 +43,18 @@
         return x_here
 
     lax.fori_loop(0, layers, up, zero, unroll=8)
+
+
+def best_scale(values, count):
+    trial = lax.broadcasted_iota(jnp.int32, (count, values[0].shape[1]), 0).astype(F32)
+    trial = 1.0 + trial * (1.0 / count)
+    inverse = 1.0 / trial
+    miss = jnp.zeros_like(trial)
+    for value in values:
+        gap = (value * inverse).astype(BF16).astype(F32) * trial - value
+        miss = miss + gap * gap
+    least = jnp.min(miss, axis=0, keepdims=True)
+    return jnp.max(jnp.where(miss == least, trial, 1.0), axis=0, keepdims=True)
 
 
 def adjoint_kernel(
@@ -95,7 +107,17 @@
 
 
 def lateral_kernel(
-    adj_ref, coef_ref, thermal_ref, received_ref, parts_ref, rhs_ref, own_ref, halo_ref, merged_ref
+    adj_ref,
+    coef_ref,
+    thermal_ref,
+    received_ref,
+    parts_ref,
+    rhs_ref,
+    own_ref,
+    halo_ref,
+    merged_ref,
+    scale_ref,
+    scaled_ref,
 ):
     step = pl.program_id(0)
     slots, nodes = adj_ref.shape
@@ -114,6 +136,16 @@
             merged_ref[k : k + 1, :] = same
         keep = 1.0 - jnp.sum(coef_ref[...], axis=0, keepdims=True)
         rhs_ref[...] = thermal_ref[...] * keep
+        for tile in range(nodes // NODE_TILE):
+            cols = pl.ds(tile * NODE_TILE, NODE_TILE)
+            merged = [merged_ref[k : k + 1, cols] for k in range(slots)]
+            scale = best_scale(merged, 64)
+            scale_ref[:, cols] = scale
+            merged_ref[:, cols] = merged_ref[:, cols] / scale
+            x = parts_ref[:layers, cols].astype(F32) + parts_ref[layers:, cols].astype(F32)
+            x_high, x_low = halves(x * scale)
+            scaled_ref[:layers, cols] = x_high
+            scaled_ref[layers:, cols] = x_low
 
     here = pl.ds(pl.multiple_of(jnp.minimum(step, own_steps - 1) * SLOT_ROWS, SLOT_ROWS), SLOT_ROWS)
     high, low = halves(thermal_ref[:, here])
@@ -123,27 +155,19 @@
     ext = jnp.concatenate([high, low], 0)
     row = lax.broadcasted_iota(jnp.int32, (SLOT_ROWS, NODE_TILE), 0).astype(F32).astype(BF16)
     total = jnp.zeros((2 * layers, SLOT_ROWS), F32)
-    fine = jnp.zeros((layers, SLOT_ROWS), F32)
     for tile in range(nodes // NODE_TILE):
         cols = pl.ds(tile * NODE_TILE, NODE_TILE)
         local = (adj_ref[:, cols] - step * SLOT_ROWS).astype(F32).astype(BF16)
-        share, rest = halves(merged_ref[:, cols])
+        share = merged_ref[:, cols].astype(BF16)
         weights = jnp.zeros((SLOT_ROWS, NODE_TILE), BF16)
-        small = jnp.zeros((SLOT_ROWS, NODE_TILE), BF16)
         for k in range(slots):
-            match = row == local[k : k + 1, :]
-            weights = jnp.where(match, share[k : k + 1, :], weights)
-            small = jnp.where(match, rest[k : k + 1, :], small)
+            weights = jnp.where(row == local[k : k + 1, :], share[k : k + 1, :], weights)
         part = jnp.dot(ext, weights, preferred_element_type=F32)
-        part = part[:layers] + part[layers:]
-        rhs_ref[:, cols] += part + jnp.dot(ext[:layers], small, preferred_element_type=F32)
+        rhs_ref[:, cols] += (part[:layers] + part[layers:]) * scale_ref[:, cols]
         total += lax.dot_general(
-            parts_ref[:, cols], weights, contract, preferred_element_type=F32
+            scaled_ref[:, cols], weights, contract, preferred_element_type=F32
         )
-        fine += lax.dot_general(
-            parts_ref[:layers, cols], small, contract, preferred_element_type=F32
-        )
-    grad = total[:layers] + total[layers:] + fine
+    grad = total[:layers] + total[layers:]
 
     @pl.when(is_own)
     def _():
@@ -187,6 +211,9 @@
     row_high = share[1:2] + share[3:4]
     col_low = share[0:1] + share[1:2]
     col_high = share[2:3] + share[3:4]
+    scale = best_scale([col_low, col_high], 64)
+    col_low = col_low / scale
+    col_high = col_high / scale
     base_row = row_ref[0:1, :]
     base_col = col_ref[0:1, :] - start_ref[0]
     base_col = jnp.where(base_col < 0, base_col + band_width, base_col)
@@ -199,10 +226,10 @@
     cols = jnp.where(
         col_at == base_col, col_low, jnp.where(col_at == base_col + 1, col_high, 0.0)
     )
-    cols_hi, cols_lo = halves(cols)
+    cols = cols.astype(BF16)
     window = window_ref[...].reshape(fields * tile_rows, window_cols)
-    mixed = jnp.dot(window, cols_hi, preferred_element_type=F32)
-    mixed = mixed + jnp.dot(window, cols_lo, preferred_element_type=F32)
+    rows = rows * scale
+    mixed = jnp.dot(window, cols, preferred_element_type=F32)
     forced = [
         jnp.sum(mixed[f * tile_rows : (f + 1) * tile_rows] * rows, axis=0, keepdims=True)
         for f in range(fields)
@@ -231,7 +258,7 @@
         lefts.append(halves(node_grad * rows))
     left_hi = jnp.concatenate([high for high, _ in lefts], 0)
     left_lo = jnp.concatenate([low for _, low in lefts], 0)
-    grad = dot(left_hi, cols_hi) + dot(left_lo, cols_hi) + dot(left_hi, cols_lo)
+    grad = dot(left_hi, cols) + dot(left_lo, cols)
     grad_ref[...] += grad.reshape(fields, tile_rows, window_cols)
 
     @pl.when(pl.program_id(0) == pl.num_programs(0) - 1)
@@ -333,7 +360,11 @@
             pl.BlockSpec((layers, SLOT_ROWS), lambda i: (0, jnp.minimum(i, own_steps - 1))),
             pl.BlockSpec((SLOT_ROWS, layers), lambda i: (jnp.maximum(i - own_steps, 0), 0)),
         ),
-        scratch_shapes=[pltpu.VMEM((slots, nodes), F32)],
+        scratch_shapes=[
+            pltpu.VMEM((slots, nodes), F32),
+            pltpu.VMEM((1, nodes), F32),
+            pltpu.VMEM((2 * layers, nodes), BF16),
+        ],
         compiler_params=params,
         cost_estimate=cost(8 * layers * nodes * extended, 8000000),
         name="lateral",

time: 115 us -> 90.4 us (0.79)
  Pallas kernels: 74.6 us -> 50.3 us
    pallas_call x1, Pallas kernels: 44 us -> 27.9 us  [per_device(): pl.pallas_call(lateral_kernel, grid=(extended // SLOT_ROWS,), out_shape=(...]
    pallas_call x1, Pallas kernels: 21.8 us -> 13.5 us  [per_device(): pl.pallas_call(functools.partial(forcing_kernel, band_width=band_width),...]
  transfers between devices with their start and end apart: 6 -> 6, of which waited for: 2 -> 2; matrix products, arithmetic and copies ran while one was open for 8% -> 10% of each run, Pallas kernels for 65% -> 56%
where the time goes in v3:
time: 90.4 us; the launch traced here: 89.9 us
  Pallas kernels  50.3 us (56%)
  starting transfers between devices  20.3 us (22%)
  local copies, waits for them, and re-layouts  7.85 us (9%)
  waiting for transfers between devices  4.45 us (5%)
  matrix products  4.12 us (5%)
  other arithmetic  2.21 us (2%)
    pallas_call x1, Pallas kernels, per_device(): pl.pallas_call(lateral_kernel, grid=(extended // SLOT_ROWS,), out_shape=(...  27.9 us
    pallas_call x1, Pallas kernels, per_device(): pl.pallas_call(functools.partial(forcing_kernel, band_width=band_width),...  13.5 us
    all_to_all x1, starting transfers between devices, per_device(): lax.all_to_all(departing.reshape(columns, halo // columns, layers), 'lon'...  7.28 us
    pallas_call x1, Pallas kernels, per_device(): pl.pallas_call(adjoint_kernel, out_shape=(jax.ShapeDtypeStruct((2 * layer...  4.86 us
    pallas_call x1, Pallas kernels, per_device(): pl.pallas_call(forward_kernel, out_shape=jax.ShapeDtypeStruct((layers, no...  4.02 us
    all_to_all x1, starting transfers between devices, per_device(): lax.all_to_all(halo_grad.reshape(columns, halo // columns, layers), 'lon'...  3.33 us
    ppermute x1, starting transfers between devices, per_device(): rim_from_right = lax.ppermute(left_rim, 'lon', downward)  2.86 us
    ppermute x1, starting transfers between devices, per_device(): from_right = lax.ppermute(atmosphere_inputs[:, :, :half], 'lon', downward)  2.77 us
  transfers between devices with their start and end apart: 6, of which 2 were waited for; matrix products, arithmetic and copies ran while one was open for 10% of the time, Pallas kernels for 56%

profile of v3, /device:TPU:0, one launch (start us, length us, event | category | flops | bytes accessed | tf_op | source)
XLA Modules:
  0.0 89.9 jit_solution(3143663593360633337)
XLA Ops:
  0.6 0.0 copy-start
  0.6 0.8 eq.17
  1.4 2.1 %fusion.3 = bf16[256,64]{0,1:T(8,128)(2,1)S(1)} fusion(s32[256]{0:T(256)S(1)} %eq.17, f32[64,4096]{1,0:T(8,128)} %thermal_ref.1), kind=kOutput, calls=%fused_computation.5 | convolution fusion | flops 135544832 | bytes 1082368 | tf_op jit(solution)/shard_map/dot_general | solution.py:309
  3.6 0.1 copy.16
  3.7 0.7 reshape.28
  4.4 7.3 %all-to-all-start = ((bf16[8,2,1024]{2,1,0:T(2,128)(2,1)}), bf16[8,2,1024]{2,1,0:T(2,128)(2,1)S(1)}, u32[]{:S(2)}, u32[]{:S(2)}) async-start(bf16[8,2,1024]{2,1,0:T(2,128)(2,1)} %reshape.28), calls=%async_computation | async-start | bytes 65536 | tf_op jit(solution)/shard_map/all_to_all | solution.py:315
  11.7 0.0 copy-done
  11.7 0.2 fusion.5
  11.9 2.1 %collective-permute-start = (bf16[9,128,64]{2,1,0:T(8,128)(2,1)S(1)}, bf16[9,128,64]{2,1,0:T(8,128)(2,1)S(1)}, u32[]{:S(2)}, u32[]{:S(2)}) collective-permute-start(bf16[9,128,64]{2,1,0:T(8,128)(2,1)S(1)} %get-tuple-element.29), channel_id=1, source_target_pairs={{0,1},{1,2},{2,3},{3,4},{4,5},{5,6},{6,7},{7,0},{8,9},{9,10},{10,1... | collective-permute-start | bytes 442376 | tf_op jit(solution)/shard_map/ppermute | solution.py:304
  13.9 2.8 %collective-permute-start.1 = (bf16[9,128,64]{2,1,0:T(8,128)(2,1)S(1)}, bf16[9,128,64]{2,1,0:T(8,128)(2,1)S(1)}, u32[]{:S(2)}, u32[]{:S(2)}) collective-permute-start(bf16[9,128,64]{2,1,0:T(8,128)(2,1)S(1)} %get-tuple-element.30), channel_id=1, source_target_pairs={{1,0},{2,1},{3,2},{4,3},{5,4},{6,5},{7,6},{0,7},{9,8},{10,9},{11,1... | collective-permute-start | bytes 442376 | tf_op jit(solution)/shard_map/ppermute | solution.py:305
  16.7 1.5 %slice.11.thermal_ref = f32[1,4096]{1,0:T(1,128)} slice(f32[64,4096]{1,0:T(8,128)} %thermal_ref.1), slice={[0:1], [0:4096]} | slice | bytes 32768 | tf_op jit(solution)/shard_map/slice | solution.py:429
  18.2 4.9 %adjoint_solve.1 = (bf16[128,4096]{1,0:T(8,128)(2,1)}, f32[1,4096]{1,0:T(1,128)}, f32[64,32,128]{2,1,0:T(8,128)}, f32[64,32,128]{2,1,0:T(8,128)}, f32[64,32,128]{2,1,0:T(8,128)}) custom-call(f32[64,4096]{1,0:T(8,128)} %mix_ref.1, f32[64,4096]{1,0:T(8,128)} %rhs_ref.1), custom_call_target="tpu_custom_call" | custom-call | flops 5242880 | bytes 6291456 | tf_op jit(solution)/shard_map/adjoint_solve/pallas_call | solution.py:325
  23.1 0.0 all-to-all-done
  23.1 0.1 reshape.29
  23.2 0.7 copy.17
  23.9 27.9 %lateral.1 = (f32[64,4096]{1,0:T(8,128)}, f32[64,4096]{1,0:T(8,128)}, bf16[256,64]{1,0:T(8,128)(2,1)}) custom-call(s32[6,4096]{1,0:T(8,128)} %adj_ref.1, f32[6,4096]{1,0:T(8,128)} %coef_ref.1, f32[64,4096]{1,0:T(8,128)} %thermal_ref.1, bf16[64,256]{1,0:T(8,128)(2,1)} %bitcast.12, bf16[128,4096]{1,0:T(8,128)(2,1)} %get-tuple-element.16.parts_ref), custom_call_target="tpu_custom_call" | custom-call | flops 9126805504 | bytes 8000000 | tf_op jit(solution)/shard_map/lateral/pallas_call | solution.py:343
  51.8 1.6 %reshape.30 = bf16[8,2,1024]{2,1,0:T(2,128)(2,1)} reshape(bf16[8,32,64]{2,1,0:T(8,128)(2,1)} %bitcast.11) | data formatting | bytes 65536
  53.4 3.3 %all-to-all-start.1 = ((bf16[8,2,1024]{2,1,0:T(2,128)(2,1)}), bf16[8,2,1024]{2,1,0:T(2,128)(2,1)S(1)}, u32[]{:S(2)}, u32[]{:S(2)}) async-start(bf16[8,2,1024]{2,1,0:T(2,128)(2,1)} %reshape.30), calls=%async_computation.1 | async-start | bytes 65536 | tf_op jit(solution)/shard_map/all_to_all | solution.py:378
  56.7 0.0 collective-permute-done
  56.7 0.0 collective-permute-done.1
  56.8 1.2 %pad_maximum_fusion.window_ref = bf16[9,128,256]{2,1,0:T(8,128)(2,1)} fusion(bf16[9,128,64]{2,1,0:T(8,128)(2,1)S(1)} %collective-permute-done.1, bf16[9,128,128]{2,1,0:T(8,128)(2,1)S(1)} %copy-done, bf16[9,128,64]{2,1,0:T(8,128)(2,1)S(1)} %collective-permute-done), kind=kLoop, calls=%fused_computation.6 | loop fusion | flops 1769472 | bytes 1179648 | tf_op jit(solution)/shard_map/concatenate | solution.py:386
  57.9 13.5 %forcing.1 = (f32[1,4096]{1,0:T(1,128)}, f32[1,4096]{1,0:T(1,128)}, f32[9,128,128]{2,1,0:T(8,128)}, f32[9,128,64]{2,1,0:T(8,128)}, f32[9,128,64]{2,1,0:T(8,128)}) custom-call(s32[1]{0:T(128)} %bitcast.3.start_ref, f32[9]{0:T(128)} %factor_ref.1, bf16[9,128,256]{2,1,0:T(8,128)(2,1)} %pad_maximum_fusion.window_ref, s32[4,4096]{1,0:T(4,128)} %row_ref.1, ...), custom_call_target="tpu_custom_call" | custom-call | flops 9663676416 | bytes 4000000 | tf_op jit(solution)/shard_map/forcing/pallas_call | solution.py:396
  71.4 0.0 copy-start.2
  71.4 1.3 %copy.18 = f32[9,128,64]{1,2,0:T(8,128)S(1)} copy(f32[9,128,64]{2,1,0:T(8,128)} %get-tuple-element.27) | data formatting | bytes 589824 | tf_op jit(solution)/shard_map/forcing/pallas_call | solution.py:396
  72.7 2.0 %collective-permute-start.2 = (f32[9,128,64]{1,2,0:T(8,128)S(1)}, f32[9,128,64]{1,2,0:T(8,128)S(1)}, u32[]{:S(2)}, u32[]{:S(2)}) collective-permute-start(f32[9,128,64]{1,2,0:T(8,128)S(1)} %copy.18), channel_id=1, source_target_pairs={{0,1},{1,2},{2,3},{3,4},{4,5},{5,6},{6,7},{7,0},{8,9},{9,10},{10,1... | collective-permute-start | bytes 884744 | tf_op jit(solution)/shard_map/ppermute | solution.py:431
  74.7 0.0 copy-done.2
  74.7 0.2 copy.19
  74.9 2.9 %collective-permute-start.3 = (f32[9,128,64]{1,2,0:T(8,128)S(1)}, f32[9,128,64]{1,2,0:T(8,128)S(1)}, u32[]{:S(2)}, u32[]{:S(2)}) collective-permute-start(f32[9,128,64]{1,2,0:T(8,128)S(1)} %copy.19), channel_id=1, source_target_pairs={{1,0},{2,1},{3,2},{4,3},{5,4},{6,5},{7,6},{0,7},{9,8},{10,9},{11,1... | collective-permute-start | bytes 884744 | tf_op jit(solution)/shard_map/ppermute | solution.py:432
  77.8 0.0 all-to-all-done.1
  77.8 0.1 reshape.31
  77.9 0.0 copy-start.1
  77.9 0.0 copy-start.4
  77.9 4.0 %forward_solve.1 = f32[64,4096]{1,0:T(8,128)} custom-call(f32[64,4096]{1,0:T(8,128)} %get-tuple-element.17.rhs_ref, f32[1,4096]{1,0:T(1,128)} %get-tuple-element.19.flux_ref, f32[64,32,128]{2,1,0:T(8,128)} %get-tuple-element.20.gain_ref, f32[64,32,128]{2,1,0:T(8,128)} %get-tuple-element.21.scale_ref, f32[64,32,128]{2,1,0:T(8,128)} %get-tuple-element.22.carry_ref), custom_call_target="tpu_custom_call" | custom-call | flops 1572864 | bytes 5242880 | tf_op jit(solution)/shard_map/forward_solve/pallas_call | solution.py:434
  81.9 0.0 copy-done.1
  81.9 0.0 copy-done.4
  81.9 2.0 %convolution_add_fusion = f32[64,4096]{1,0:T(8,128)} fusion(bf16[256,64]{1,0:T(8,128)(2,1)S(1)} %bitcast.8, s32[256]{0:T(256)S(1)} %eq.17, f32[64,4096]{1,0:T(8,128)S(1)} %copy-done.1, f32[4096]{0:T(1024)S(1)} %bitcast.13, pred[64]{0:T(512)(128)(4,1)S(1)} %iota_compare_fusion.5), kind=kOutput, calls=%fused_computation | convolution fusion | flops 136052736 | bytes 2147392 | tf_op jit(solution)/shard_map/dot_general | solution.py:445
  83.9 0.0 copy-start.3
  83.9 2.2 %collective-permute-done.2 = f32[9,128,64]{1,2,0:T(8,128)S(1)} collective-permute-done((f32[9,128,64]{1,2,0:T(8,128)S(1)}, f32[9,128,64]{1,2,0:T(8,128)S(1)}, u32[]{:S(2)}, u32[]{:S(2)}) %collective-permute-start.2) | collective-permute-done | bytes 294944 | tf_op jit(solution)/shard_map/ppermute | solution.py:431
  86.2 0.2 copy.20
  86.4 2.2 %collective-permute-done.3 = f32[9,128,64]{1,2,0:T(8,128)S(1)} collective-permute-done((f32[9,128,64]{1,2,0:T(8,128)S(1)}, f32[9,128,64]{1,2,0:T(8,128)S(1)}, u32[]{:S(2)}, u32[]{:S(2)}) %collective-permute-start.3) | collective-permute-done | bytes 294944 | tf_op jit(solution)/shard_map/ppermute | solution.py:432
  88.6 0.2 copy.21
  88.9 0.0 copy-done.3
  88.9 1.0 %maximum_add_fusion = f32[9,128,128]{2,1,0:T(8,128)} fusion(f32[9,128,128]{2,1,0:T(8,128)S(1)} %copy-done.3, f32[9,128,64]{2,1,0:T(8,128)S(1)} %copy.21, f32[9,128,64]{2,1,0:T(8,128)S(1)} %copy.20), kind=kLoop, calls=%fused_computation.7 | loop fusion | flops 294912 | bytes 1769472 | tf_op jit(solution)/shard_map/add | solution.py:450
  (1 shorter events, 0.0 us)
Async XLA Ops:
  0.6 11.1 %copy-start = (bf16[9,128,128]{2,1,0:T(8,128)(2,1)S(1)}, bf16[9,128,128]{2,1,0:T(8,128)(2,1)}, u32[]{:S(2)}) copy-start(bf16[9,128,128]{2,1,0:T(8,128)(2,1)} %param.11) | copy-start | bytes 884740
  4.4 18.7 %all-to-all-start = ((bf16[8,2,1024]{2,1,0:T(2,128)(2,1)}), bf16[8,2,1024]{2,1,0:T(2,128)(2,1)S(1)}, u32[]{:S(2)}, u32[]{:S(2)}) async-start(bf16[8,2,1024]{2,1,0:T(2,128)(2,1)} %reshape.28), calls=%async_computation | async-start | bytes 65536 | tf_op jit(solution)/shard_map/all_to_all | solution.py:315
  11.9 44.9 %collective-permute-start = (bf16[9,128,64]{2,1,0:T(8,128)(2,1)S(1)}, bf16[9,128,64]{2,1,0:T(8,128)(2,1)S(1)}, u32[]{:S(2)}, u32[]{:S(2)}) collective-permute-start(bf16[9,128,64]{2,1,0:T(8,128)(2,1)S(1)} %get-tuple-element.29), channel_id=1, source_target_pairs={{0,1},{1,2},{2,3},{3,4},{4,5},{5,6},{6,7},{7,0},{8,9},{9,10},{10,1... | collective-permute-start | bytes 442376 | tf_op jit(solution)/shard_map/ppermute | solution.py:304
  13.9 42.8 %collective-permute-start.1 = (bf16[9,128,64]{2,1,0:T(8,128)(2,1)S(1)}, bf16[9,128,64]{2,1,0:T(8,128)(2,1)S(1)}, u32[]{:S(2)}, u32[]{:S(2)}) collective-permute-start(bf16[9,128,64]{2,1,0:T(8,128)(2,1)S(1)} %get-tuple-element.30), channel_id=1, source_target_pairs={{1,0},{2,1},{3,2},{4,3},{5,4},{6,5},{7,6},{0,7},{9,8},{10,9},{11,1... | collective-permute-start | bytes 442376 | tf_op jit(solution)/shard_map/ppermute | solution.py:305
  53.4 24.4 %all-to-all-start.1 = ((bf16[8,2,1024]{2,1,0:T(2,128)(2,1)}), bf16[8,2,1024]{2,1,0:T(2,128)(2,1)S(1)}, u32[]{:S(2)}, u32[]{:S(2)}) async-start(bf16[8,2,1024]{2,1,0:T(2,128)(2,1)} %reshape.30), calls=%async_computation.1 | async-start | bytes 65536 | tf_op jit(solution)/shard_map/all_to_all | solution.py:378
  71.4 3.3 %copy-start.2 = (f32[9,128,64]{2,1,0:T(8,128)S(1)}, f32[9,128,64]{2,1,0:T(8,128)}, u32[]{:S(2)}) copy-start(f32[9,128,64]{2,1,0:T(8,128)} %get-tuple-element.28) | copy-start | bytes 884740
  72.7 13.4 %collective-permute-start.2 = (f32[9,128,64]{1,2,0:T(8,128)S(1)}, f32[9,128,64]{1,2,0:T(8,128)S(1)}, u32[]{:S(2)}, u32[]{:S(2)}) collective-permute-start(f32[9,128,64]{1,2,0:T(8,128)S(1)} %copy.18), channel_id=1, source_target_pairs={{0,1},{1,2},{2,3},{3,4},{4,5},{5,6},{6,7},{7,0},{8,9},{9,10},{10,1... | collective-permute-start | bytes 884744 | tf_op jit(solution)/shard_map/ppermute | solution.py:431
  74.9 13.7 %collective-permute-start.3 = (f32[9,128,64]{1,2,0:T(8,128)S(1)}, f32[9,128,64]{1,2,0:T(8,128)S(1)}, u32[]{:S(2)}, u32[]{:S(2)}) collective-permute-start(f32[9,128,64]{1,2,0:T(8,128)S(1)} %copy.19), channel_id=1, source_target_pairs={{1,0},{2,1},{3,2},{4,3},{5,4},{6,5},{7,6},{0,7},{9,8},{10,9},{11,1... | collective-permute-start | bytes 884744 | tf_op jit(solution)/shard_map/ppermute | solution.py:432
  77.9 4.0 %copy-start.1 = (f32[64,4096]{1,0:T(8,128)S(1)}, f32[64,4096]{1,0:T(8,128)}, u32[]{:S(2)}) copy-start(f32[64,4096]{1,0:T(8,128)} %get-tuple-element.23) | copy-start | bytes 3145732
  77.9 4.0 %copy-start.4 = (f32[1,4096]{1,0:T(1,128)S(1)}, f32[1,4096]{1,0:T(1,128)}, u32[]{:S(2)}) copy-start(f32[1,4096]{1,0:T(1,128)} %get-tuple-element.24) | copy-start | bytes 49156
  83.9 4.9 %copy-start.3 = (f32[9,128,128]{2,1,0:T(8,128)S(1)}, f32[9,128,128]{2,1,0:T(8,128)}, u32[]{:S(2)}) copy-start(f32[9,128,128]{2,1,0:T(8,128)} %get-tuple-element.26) | copy-start | bytes 1769476

commit v4 on v3

--- a/solution.py
+++ b/solution.py
@@ -199,7 +199,7 @@
     band_width,
 ):
     fields, tile_rows, window_cols = grad_ref.shape
-    half = left_ref.shape[2]
+    half = left_ref.shape[1]
     tile = row_ref.shape[1]
 
     @pl.when(pl.program_id(0) == 0)
@@ -265,8 +265,8 @@
     def _():
         for f in range(fields):
             grad = grad_ref[f]
-            left_ref[f] = grad[:, :half]
-            right_ref[f] = grad[:, window_cols - half :]
+            left_ref[f] = grad[:, :half].T
+            right_ref[f] = grad[:, window_cols - half :].T
             own_ref[f] = grad[:, half : window_cols - half]
 
 
@@ -390,6 +390,8 @@
     def all_of(width):
         return pl.BlockSpec((fields, tile_rows, width), lambda i: (0, 0, 0))
 
+    rim = pl.BlockSpec((fields, half, tile_rows), lambda i: (0, 0, 0))
+
     def grid_shape(width):
         return jax.ShapeDtypeStruct((fields, tile_rows, width), F32)
 
@@ -400,8 +402,8 @@
             jax.ShapeDtypeStruct((1, nodes), F32),
             jax.ShapeDtypeStruct((1, nodes), F32),
             grid_shape(tile_cols),
-            grid_shape(half),
-            grid_shape(half),
+            jax.ShapeDtypeStruct((fields, half, tile_rows), F32),
+            jax.ShapeDtypeStruct((fields, half, tile_rows), F32),
         ),
         in_specs=[
             pl.BlockSpec(memory_space=pltpu.SMEM),
@@ -413,7 +415,7 @@
             line,
             line,
         ],
-        out_specs=(line, line, all_of(tile_cols), all_of(half), all_of(half)),
+        out_specs=(line, line, all_of(tile_cols)) + (rim,) * 2,
         scratch_shapes=[pltpu.VMEM((fields, tile_rows, window_cols), F32)],
         compiler_params=params,
         cost_estimate=cost(8 * fields * tile_rows * window_cols * nodes, 4000000),
@@ -447,7 +449,8 @@
     )
     top = lax.broadcasted_iota(jnp.int32, (layers, nodes), 0) == 0
     temp_grad = own_grad + jnp.where(top, corr, 0.0) + returned
-    forcing_grad = own_forcing + jnp.concatenate([rim_from_left, rim_from_right], 2)
+    rims = jnp.concatenate([rim_from_left, rim_from_right], 1)
+    forcing_grad = own_forcing + rims.transpose(0, 2, 1)
     return (updated_warmth, temp_grad, forcing_grad)
 
 

time: 90.4 us -> 89 us (0.985)
  other arithmetic: 2.21 us -> 1.23 us
    unnamed x14 -> x11, local copies, waits for them, and re-layouts: 2.54 us -> 3.58 us
    add x1, other arithmetic: 1.04 us -> 0.06 us  [per_device(): forcing_grad = own_forcing + rims.transpose(0, 2, 1)]
  transfers between devices with their start and end apart: 6 -> 6, of which waited for: 2 -> 2; matrix products, arithmetic and copies ran while one was open for 10% -> 10% of each run, Pallas kernels for 56% -> 57%
where the time goes in v4:
time: 89 us; the launch traced here: 88.5 us
  Pallas kernels  50.4 us (57%)
  starting transfers between devices  20.2 us (23%)
  local copies, waits for them, and re-layouts  8.17 us (9%)
  matrix products  4.12 us (5%)
  waiting for transfers between devices  3.59 us (4%)
  other arithmetic  1.23 us (1%)
    pallas_call x1, Pallas kernels, per_device(): pl.pallas_call(lateral_kernel, grid=(extended // SLOT_ROWS,), out_shape=(...  27.9 us
    pallas_call x1, Pallas kernels, per_device(): pl.pallas_call(functools.partial(forcing_kernel, band_width=band_width),...  13.6 us
    all_to_all x1, starting transfers between devices, per_device(): lax.all_to_all(departing.reshape(columns, halo // columns, layers), 'lon'...  7.28 us
    pallas_call x1, Pallas kernels, per_device(): pl.pallas_call(adjoint_kernel, out_shape=(jax.ShapeDtypeStruct((2 * layer...  4.86 us
    pallas_call x1, Pallas kernels, per_device(): pl.pallas_call(forward_kernel, out_shape=jax.ShapeDtypeStruct((layers, no...  4.02 us
    unnamed x11, local copies, waits for them, and re-layouts  3.58 us
    all_to_all x1, starting transfers between devices, per_device(): lax.all_to_all(halo_grad.reshape(columns, halo // columns, layers), 'lon'...  3.34 us
    ppermute x1, starting transfers between devices, per_device(): rim_from_right = lax.ppermute(left_rim, 'lon', downward)  2.8 us
  transfers between devices with their start and end apart: 6, of which 2 were waited for; matrix products, arithmetic and copies ran while one was open for 10% of the time, Pallas kernels for 57%

profile of v4, /device:TPU:0, one launch (start us, length us, event | category | flops | bytes accessed | tf_op | source)
XLA Modules:
  0.0 88.5 jit_solution(4436732502856860620)
XLA Ops:
  0.6 0.0 copy-start
  0.6 0.8 eq.17
  1.4 2.1 %fusion.3 = bf16[256,64]{0,1:T(8,128)(2,1)S(1)} fusion(s32[256]{0:T(256)S(1)} %eq.17, f32[64,4096]{1,0:T(8,128)} %thermal_ref.1), kind=kOutput, calls=%fused_computation.5 | convolution fusion | flops 135544832 | bytes 1082368 | tf_op jit(solution)/shard_map/dot_general | solution.py:309
  3.6 0.1 copy.16
  3.7 0.7 reshape.28
  4.4 7.3 %all-to-all-start = ((bf16[8,2,1024]{2,1,0:T(2,128)(2,1)}), bf16[8,2,1024]{2,1,0:T(2,128)(2,1)S(1)}, u32[]{:S(2)}, u32[]{:S(2)}) async-start(bf16[8,2,1024]{2,1,0:T(2,128)(2,1)} %reshape.28), calls=%async_computation | async-start | bytes 65536 | tf_op jit(solution)/shard_map/all_to_all | solution.py:315
  11.7 0.0 copy-done
  11.7 0.2 fusion.6
  11.9 2.1 %collective-permute-start = (bf16[9,128,64]{2,1,0:T(8,128)(2,1)S(1)}, bf16[9,128,64]{2,1,0:T(8,128)(2,1)S(1)}, u32[]{:S(2)}, u32[]{:S(2)}) collective-permute-start(bf16[9,128,64]{2,1,0:T(8,128)(2,1)S(1)} %get-tuple-element.35), channel_id=1, source_target_pairs={{0,1},{1,2},{2,3},{3,4},{4,5},{5,6},{6,7},{7,0},{8,9},{9,10},{10,1... | collective-permute-start | bytes 442376 | tf_op jit(solution)/shard_map/ppermute | solution.py:304
  13.9 2.8 %collective-permute-start.1 = (bf16[9,128,64]{2,1,0:T(8,128)(2,1)S(1)}, bf16[9,128,64]{2,1,0:T(8,128)(2,1)S(1)}, u32[]{:S(2)}, u32[]{:S(2)}) collective-permute-start(bf16[9,128,64]{2,1,0:T(8,128)(2,1)S(1)} %get-tuple-element.36), channel_id=1, source_target_pairs={{1,0},{2,1},{3,2},{4,3},{5,4},{6,5},{7,6},{0,7},{9,8},{10,9},{11,1... | collective-permute-start | bytes 442376 | tf_op jit(solution)/shard_map/ppermute | solution.py:305
  16.7 1.5 %slice.11.thermal_ref = f32[1,4096]{1,0:T(1,128)} slice(f32[64,4096]{1,0:T(8,128)} %thermal_ref.1), slice={[0:1], [0:4096]} | slice | bytes 32768 | tf_op jit(solution)/shard_map/slice | solution.py:431
  18.2 4.9 %adjoint_solve.1 = (bf16[128,4096]{1,0:T(8,128)(2,1)}, f32[1,4096]{1,0:T(1,128)}, f32[64,32,128]{2,1,0:T(8,128)}, f32[64,32,128]{2,1,0:T(8,128)}, f32[64,32,128]{2,1,0:T(8,128)}) custom-call(f32[64,4096]{1,0:T(8,128)} %mix_ref.1, f32[64,4096]{1,0:T(8,128)} %rhs_ref.1), custom_call_target="tpu_custom_call" | custom-call | flops 5242880 | bytes 6291456 | tf_op jit(solution)/shard_map/adjoint_solve/pallas_call | solution.py:325
  23.1 0.0 all-to-all-done
  23.1 0.1 reshape.29
  23.2 0.7 copy.17
  23.9 27.9 %lateral.1 = (f32[64,4096]{1,0:T(8,128)}, f32[64,4096]{1,0:T(8,128)}, bf16[256,64]{1,0:T(8,128)(2,1)}) custom-call(s32[6,4096]{1,0:T(8,128)} %adj_ref.1, f32[6,4096]{1,0:T(8,128)} %coef_ref.1, f32[64,4096]{1,0:T(8,128)} %thermal_ref.1, bf16[64,256]{1,0:T(8,128)(2,1)} %bitcast.16, bf16[128,4096]{1,0:T(8,128)(2,1)} %get-tuple-element.16.parts_ref), custom_call_target="tpu_custom_call" | custom-call | flops 9126805504 | bytes 8000000 | tf_op jit(solution)/shard_map/lateral/pallas_call | solution.py:343
  51.9 1.6 %reshape.30 = bf16[8,2,1024]{2,1,0:T(2,128)(2,1)} reshape(bf16[8,32,64]{2,1,0:T(8,128)(2,1)} %bitcast.15) | data formatting | bytes 65536
  53.4 3.3 %all-to-all-start.1 = ((bf16[8,2,1024]{2,1,0:T(2,128)(2,1)}), bf16[8,2,1024]{2,1,0:T(2,128)(2,1)S(1)}, u32[]{:S(2)}, u32[]{:S(2)}) async-start(bf16[8,2,1024]{2,1,0:T(2,128)(2,1)} %reshape.30), calls=%async_computation.1 | async-start | bytes 65536 | tf_op jit(solution)/shard_map/all_to_all | solution.py:378
  56.8 0.0 collective-permute-done
  56.8 0.0 collective-permute-done.1
  56.8 1.2 %pad_maximum_fusion.window_ref = bf16[9,128,256]{2,1,0:T(8,128)(2,1)} fusion(bf16[9,128,64]{2,1,0:T(8,128)(2,1)S(1)} %collective-permute-done.1, bf16[9,128,128]{2,1,0:T(8,128)(2,1)S(1)} %copy-done, bf16[9,128,64]{2,1,0:T(8,128)(2,1)S(1)} %collective-permute-done), kind=kLoop, calls=%fused_computation.6 | loop fusion | flops 1769472 | bytes 1179648 | tf_op jit(solution)/shard_map/concatenate | solution.py:386
  58.0 13.6 %forcing.1 = (f32[1,4096]{1,0:T(1,128)}, f32[1,4096]{1,0:T(1,128)}, f32[9,128,128]{2,1,0:T(8,128)}, f32[9,64,128]{2,1,0:T(8,128)}, f32[9,64,128]{2,1,0:T(8,128)}) custom-call(s32[1]{0:T(128)} %bitcast.3.start_ref, f32[9]{0:T(128)} %factor_ref.1, bf16[9,128,256]{2,1,0:T(8,128)(2,1)} %pad_maximum_fusion.window_ref, s32[4,4096]{1,0:T(4,128)} %row_ref.1, ...), custom_call_target="tpu_custom_call" | custom-call | flops 9663676416 | bytes 4000000 | tf_op jit(solution)/shard_map/forcing/pallas_call | solution.py:398
  71.6 2.0 %collective-permute-start.2 = (f32[9,64,128]{2,1,0:T(8,128)}, f32[9,64,128]{2,1,0:T(8,128)S(1)}, u32[]{:S(2)}, u32[]{:S(2)}) collective-permute-start(f32[9,64,128]{2,1,0:T(8,128)} %get-tuple-element.27), channel_id=1, source_target_pairs={{0,1},{1,2},{2,3},{3,4},{4,5},{5,6},{6,7},{7,0},{8,9},{9,10},{10,1... | collective-permute-start | bytes 884744 | tf_op jit(solution)/shard_map/ppermute | solution.py:433
  73.5 2.8 %collective-permute-start.3 = (f32[9,64,128]{2,1,0:T(8,128)}, f32[9,64,128]{2,1,0:T(8,128)S(1)}, u32[]{:S(2)}, u32[]{:S(2)}) collective-permute-start(f32[9,64,128]{2,1,0:T(8,128)} %get-tuple-element.28), channel_id=1, source_target_pairs={{1,0},{2,1},{3,2},{4,3},{5,4},{6,5},{7,6},{0,7},{9,8},{10,9},{11,1... | collective-permute-start | bytes 884744 | tf_op jit(solution)/shard_map/ppermute | solution.py:434
  76.3 0.0 all-to-all-done.1
  76.4 0.1 reshape.31
  76.5 1.3 %copy.18 = f32[9,128,128]{1,2,0:T(8,128)S(1)} copy(f32[9,128,128]{2,1,0:T(8,128)} %get-tuple-element.26) | data formatting | bytes 1179648 | tf_op jit(solution)/shard_map/forcing/pallas_call | solution.py:398
  77.8 0.0 copy-start.1
  77.8 0.0 copy-start.2
  77.8 4.0 %forward_solve.1 = f32[64,4096]{1,0:T(8,128)} custom-call(f32[64,4096]{1,0:T(8,128)} %get-tuple-element.17.rhs_ref, f32[1,4096]{1,0:T(1,128)} %get-tuple-element.19.flux_ref, f32[64,32,128]{2,1,0:T(8,128)} %get-tuple-element.20.gain_ref, f32[64,32,128]{2,1,0:T(8,128)} %get-tuple-element.21.scale_ref, f32[64,32,128]{2,1,0:T(8,128)} %get-tuple-element.22.carry_ref), custom_call_target="tpu_custom_call" | custom-call | flops 1572864 | bytes 5242880 | tf_op jit(solution)/shard_map/forward_solve/pallas_call | solution.py:436
  81.8 0.0 copy-done.1
  81.8 0.0 copy-done.2
  81.8 2.0 %convolution_add_fusion = f32[64,4096]{1,0:T(8,128)} fusion(bf16[256,64]{1,0:T(8,128)(2,1)S(1)} %bitcast.12, s32[256]{0:T(256)S(1)} %eq.17, f32[64,4096]{1,0:T(8,128)S(1)} %copy-done.1, f32[4096]{0:T(1024)S(1)} %bitcast.17, pred[64]{0:T(512)(128)(4,1)S(1)} %iota_compare_fusion.5), kind=kOutput, calls=%fused_computation | convolution fusion | flops 136052736 | bytes 2147392 | tf_op jit(solution)/shard_map/dot_general | solution.py:447
  83.8 1.5 %collective-permute-done.2 = f32[9,64,128]{2,1,0:T(8,128)S(1)} collective-permute-done((f32[9,64,128]{2,1,0:T(8,128)}, f32[9,64,128]{2,1,0:T(8,128)S(1)}, u32[]{:S(2)}, u32[]{:S(2)}) %collective-permute-start.2) | collective-permute-done | bytes 294944 | tf_op jit(solution)/shard_map/ppermute | solution.py:433
  85.3 2.1 %collective-permute-done.3 = f32[9,64,128]{2,1,0:T(8,128)S(1)} collective-permute-done((f32[9,64,128]{2,1,0:T(8,128)}, f32[9,64,128]{2,1,0:T(8,128)S(1)}, u32[]{:S(2)}, u32[]{:S(2)}) %collective-permute-start.3) | collective-permute-done | bytes 294944 | tf_op jit(solution)/shard_map/ppermute | solution.py:434
  87.4 0.1 fusion.4
  87.5 1.1 %copy.19 = f32[9,128,128]{2,1,0:T(8,128)} copy(f32[9,128,128]{1,2,0:T(8,128)S(1)} %fusion.4) | data formatting | bytes 1179648
  (1 shorter events, 0.0 us)
Async XLA Ops:
  0.6 11.1 %copy-start = (bf16[9,128,128]{2,1,0:T(8,128)(2,1)S(1)}, bf16[9,128,128]{2,1,0:T(8,128)(2,1)}, u32[]{:S(2)}) copy-start(bf16[9,128,128]{2,1,0:T(8,128)(2,1)} %param.11) | copy-start | bytes 884740
  4.4 18.7 %all-to-all-start = ((bf16[8,2,1024]{2,1,0:T(2,128)(2,1)}), bf16[8,2,1024]{2,1,0:T(2,128)(2,1)S(1)}, u32[]{:S(2)}, u32[]{:S(2)}) async-start(bf16[8,2,1024]{2,1,0:T(2,128)(2,1)} %reshape.28), calls=%async_computation | async-start | bytes 65536 | tf_op jit(solution)/shard_map/all_to_all | solution.py:315
  11.9 44.9 %collective-permute-start = (bf16[9,128,64]{2,1,0:T(8,128)(2,1)S(1)}, bf16[9,128,64]{2,1,0:T(8,128)(2,1)S(1)}, u32[]{:S(2)}, u32[]{:S(2)}) collective-permute-start(bf16[9,128,64]{2,1,0:T(8,128)(2,1)S(1)} %get-tuple-element.35), channel_id=1, source_target_pairs={{0,1},{1,2},{2,3},{3,4},{4,5},{5,6},{6,7},{7,0},{8,9},{9,10},{10,1... | collective-permute-start | bytes 442376 | tf_op jit(solution)/shard_map/ppermute | solution.py:304
  13.9 42.8 %collective-permute-start.1 = (bf16[9,128,64]{2,1,0:T(8,128)(2,1)S(1)}, bf16[9,128,64]{2,1,0:T(8,128)(2,1)S(1)}, u32[]{:S(2)}, u32[]{:S(2)}) collective-permute-start(bf16[9,128,64]{2,1,0:T(8,128)(2,1)S(1)} %get-tuple-element.36), channel_id=1, source_target_pairs={{1,0},{2,1},{3,2},{4,3},{5,4},{6,5},{7,6},{0,7},{9,8},{10,9},{11,1... | collective-permute-start | bytes 442376 | tf_op jit(solution)/shard_map/ppermute | solution.py:305
  53.4 22.9 %all-to-all-start.1 = ((bf16[8,2,1024]{2,1,0:T(2,128)(2,1)}), bf16[8,2,1024]{2,1,0:T(2,128)(2,1)S(1)}, u32[]{:S(2)}, u32[]{:S(2)}) async-start(bf16[8,2,1024]{2,1,0:T(2,128)(2,1)} %reshape.30), calls=%async_computation.1 | async-start | bytes 65536 | tf_op jit(solution)/shard_map/all_to_all | solution.py:378
  71.6 13.7 %collective-permute-start.2 = (f32[9,64,128]{2,1,0:T(8,128)}, f32[9,64,128]{2,1,0:T(8,128)S(1)}, u32[]{:S(2)}, u32[]{:S(2)}) collective-permute-start(f32[9,64,128]{2,1,0:T(8,128)} %get-tuple-element.27), channel_id=1, source_target_pairs={{0,1},{1,2},{2,3},{3,4},{4,5},{5,6},{6,7},{7,0},{8,9},{9,10},{10,1... | collective-permute-start | bytes 884744 | tf_op jit(solution)/shard_map/ppermute | solution.py:433
  73.5 13.9 %collective-permute-start.3 = (f32[9,64,128]{2,1,0:T(8,128)}, f32[9,64,128]{2,1,0:T(8,128)S(1)}, u32[]{:S(2)}, u32[]{:S(2)}) collective-permute-start(f32[9,64,128]{2,1,0:T(8,128)} %get-tuple-element.28), channel_id=1, source_target_pairs={{1,0},{2,1},{3,2},{4,3},{5,4},{6,5},{7,6},{0,7},{9,8},{10,9},{11,1... | collective-permute-start | bytes 884744 | tf_op jit(solution)/shard_map/ppermute | solution.py:434
  77.8 4.0 %copy-start.1 = (f32[64,4096]{1,0:T(8,128)S(1)}, f32[64,4096]{1,0:T(8,128)}, u32[]{:S(2)}) copy-start(f32[64,4096]{1,0:T(8,128)} %get-tuple-element.23) | copy-start | bytes 3145732
  77.8 4.0 %copy-start.2 = (f32[1,4096]{1,0:T(1,128)S(1)}, f32[1,4096]{1,0:T(1,128)}, u32[]{:S(2)}) copy-start(f32[1,4096]{1,0:T(1,128)} %get-tuple-element.24) | copy-start | bytes 49156
